TPU v7x, 32 devices: a whole 2x2x4 slice. The times are simulated.
32 devices in a mesh: groups: 2 (over y), ctx: 16 (over z, x, core).
Axes of the slice: x: 2, y: 2, z: 4, core: 2. Of those that a mesh axis runs over, the one named last changes fastest.
Arguments:
- features: bfloat16 [12288, 5760], P(('groups', 'ctx')), parts along dimension 0, may hold values from -6 to 6
- positions: int32 [12288], P(('groups', 'ctx')), parts along dimension 0, may hold values from 0 to 4095, as said below
- counts: int32 [32], P(('groups', 'ctx')), parts along dimension 0, may hold values from 128 to 384, as said below
- conv_weight: float32 [3, 5760], replicated, may hold values from -3.5 to 3.5
- pole_rate: float32 [16, 1920], replicated, may hold values from 4.8828125e-05 to 0.15
- pole_residue: float32 [16, 1920], replicated, may hold values from -0.5 to 0.5
- skip_gain: float32 [1920], replicated, may hold values from 0.5 to 1.5
- out_weight: bfloat16 [1920, 1920], replicated, may hold values from -0.125 to 0.125
Outputs:
- block_out: bfloat16 [8192, 1920], P(('groups', 'ctx')), parts along dimension 0
There are 2 independent parts, one for each index of `groups`. A program takes and returns all parts, laid end to end along the dimension named above; an argument that names none is the same for every part. Nothing has to cross between parts.
Inputs may be any that keep to these rules, and one draw needn't show every extreme that they name: Among the live slots of all sampler devices every position 0 to 4095 stands exactly once; the owner of a position is position // 256; at most 32 live slots of one sampler device have the same owner, and some sampler device has exactly 32 for some owner; slots that are not live hold arbitrary positions. The counts sum to 4096; at least one device has exactly 384 and at least one exactly 128.
All inputs are finite; a program needn't handle non-finite values.
Results may differ from a plain program's by a relative error of at most 0.0051.
Values may be sent and summed in bfloat16 or wider, within the bound.
A program may use at most 128 MiB of HBM per device.

v0:
```python
import functools

import jax
import jax.numpy as jnp
from jax import lax
from jax.experimental import pallas as pl
from jax.experimental.pallas import tpu as pltpu
from jax.sharding import PartitionSpec as P

LANES = 128
ROWS = 8
MESH = pl.DeviceIdType.MESH
f32, bf16 = jnp.float32, jnp.bfloat16

block_len = 32


def from_behind(array, axis, by):
    count = lax.axis_size(axis)
    pairs = [(i, i + by) for i in range(count) if 0 <= i + by < count]
    return lax.ppermute(array, axis, pairs)


def plain_on_device(
    features, positions, counts, conv_weight, pole_rate, pole_residue, skip_gain, out_weight
):
    devices = lax.axis_size("ctx")
    slot_count = features.shape[0]
    feat_width = features.shape[1]
    channels = feat_width // 3
    tok_rows = 2 * slot_count // 3
    pair_cap = 2 * tok_rows // devices
    taps = conv_weight.shape[0]
    poles = pole_rate.shape[0]
    slot_ids = jnp.arange(slot_count, dtype=jnp.int32)
    is_live = slot_ids < counts[0]
    owners = jnp.where(is_live, positions // tok_rows, devices)
    owner_hot = (owners[:, None] == jnp.arange(devices, dtype=jnp.int32)[None, :]).astype(jnp.int32)
    within = jnp.sum(jnp.cumsum(owner_hot, axis=0) * owner_hot, axis=1) - 1
    flat_index = jnp.where(is_live, owners * pair_cap + within, devices * pair_cap)
    outbox = (
        jnp.zeros((devices * pair_cap + 1, feat_width), features.dtype)
        .at[flat_index]
        .set(features)[:-1]
    )
    local_pos = (
        jnp.full((devices * pair_cap + 1,), -1, jnp.int32)
        .at[flat_index]
        .set(positions % tok_rows)[:-1]
    )
    outbox = outbox.reshape(devices, pair_cap, feat_width)
    local_pos = local_pos.reshape(devices, pair_cap)
    arrived, arrived_pos = (
        lax.all_to_all(outbox, "ctx", split_axis=0, concat_axis=0, tiled=True),
        lax.all_to_all(local_pos, "ctx", split_axis=0, concat_axis=0, tiled=True),
    )
    target = jnp.where(arrived_pos >= 0, arrived_pos, tok_rows).reshape(-1)
    placed = (
        jnp.zeros((tok_rows + 1, feat_width), features.dtype)
        .at[target]
        .set(arrived.reshape(-1, feat_width))[:-1]
    )
    rim_rows = from_behind(placed[tok_rows - (taps - 1) :], "ctx", 1)
    extended = jnp.concatenate([rim_rows, placed], axis=0)
    featured = jnp.zeros((tok_rows, feat_width), jnp.float32)
    for tap in range(taps):
        start = taps - 1 - tap
        featured = featured + conv_weight[tap][None, :] * extended[start : start + tok_rows].astype(
            jnp.float32
        )
    query_feat = featured[:, :channels]
    product = featured[:, channels : 2 * channels] * featured[:, 2 * channels :]
    num_blocks = tok_rows // block_len
    lag_steps = jnp.arange(block_len + 1).astype(jnp.float32)
    powers = jnp.exp(-pole_rate[None] * lag_steps[:, None, None])
    filter_taps = jnp.sum(powers[:block_len] * pole_residue[None], axis=1)
    blocked = product.reshape(num_blocks, block_len, channels)
    padded_blk = jnp.pad(blocked, ((0, 0), (block_len - 1, 0), (0, 0)))
    inside = jnp.zeros((num_blocks, block_len, channels), jnp.float32)
    for lag in range(block_len):
        first = block_len - 1 - lag
        inside = inside + filter_taps[lag][None, None, :] * padded_blk[:, first : first + block_len]
    blk_sums = jnp.zeros((num_blocks, poles, channels), jnp.float32)
    for row in range(block_len):
        blk_sums = blk_sums + powers[block_len - 1 - row][None] * blocked[:, row][:, None, :]
    decay_blk = powers[block_len]

    def advance(running, block_sum):
        return (decay_blk * running + block_sum, running)

    local_end, starts = lax.scan(advance, jnp.zeros((poles, channels), jnp.float32), blk_sums)
    decay_dev = jnp.exp(-pole_rate * float(tok_rows))

    def relay_step(counter, incoming):
        return from_behind(decay_dev * incoming + local_end, "ctx", 1)

    carry_in = lax.fori_loop(0, devices - 1, relay_step, jnp.zeros_like(local_end))
    block_starts = (jnp.arange(num_blocks) * block_len).astype(jnp.float32)
    block_decay = jnp.exp(-pole_rate[None] * block_starts[:, None, None])
    incoming = starts + block_decay * carry_in[None]
    inward = pole_residue[None] * powers[1:]
    from_state = jnp.zeros((num_blocks, block_len, channels), jnp.float32)
    for pole in range(poles):
        from_state = from_state + inward[:, pole][None] * incoming[:, pole][:, None, :]
    convolved = (inside + from_state).reshape(tok_rows, channels)
    filtered = skip_gain[None, :] * product + convolved
    gated_rows = (query_feat * filtered).astype(jnp.bfloat16)
    return jnp.dot(gated_rows, out_weight, preferred_element_type=jnp.float32).astype(jnp.bfloat16)

def col_tile(width):
    for tile in (384, 256, 128):
        if width % tile == 0:
            return tile
    return width


def scan_spans(n):
    spans, span = [], 1
    while span < n:
        spans.append(span)
        span *= 4
    return spans


def mega(
    n, cap, tok, up_front,
    counts, feats_hbm, pos, convw, rate, resid, skip, w_hbm, out,
    box_kv, box_q, arr_kv, arr_q, hot_s, place_s, prod, filt, gated, natural, state,
    feats, decay, rim_kv_out, rim_kv_in, rim_q_out, rim_q_in, own, acc, tx, rx, w_vmem,
    send_kv, recv_kv, send_q, recv_q, rim_sems, scan_send, scan_recv, self_sems, w_sem, f_sems,
):
    me = lax.axis_index("ctx")
    slots, feat = feats_hbm.shape
    ch = feat // 3
    poles = rate.shape[0]
    steps = tok // ROWS
    tile = col_tile(ch)
    rows = n * cap
    barrier = pltpu.get_barrier_semaphore()

    bits = (n - 1).bit_length()

    def mask_of(d):
        return sum(((d // (1 << b)) % 2) * (1 << (bits - 1 - b)) for b in range(bits))

    def peer_of(d):
        m = mask_of(d)
        return sum(((me // (1 << b) + m // (1 << b)) % 2) * (1 << b) for b in range(bits))

    def greet(d, c):
        pl.semaphore_signal(barrier, inc=1, device_id={"ctx": peer_of(d)}, device_id_type=MESH)
        return c

    lax.fori_loop(1, n, greet, 0)
    kv_cols = pl.ds(ch, 2 * ch)
    f_kv = pltpu.make_async_copy(feats_hbm.at[:, kv_cols], feats.at[:, kv_cols], f_sems.at[0])
    f_q = pltpu.make_async_copy(feats_hbm.at[:, pl.ds(0, ch)], feats.at[:, pl.ds(0, ch)], f_sems.at[1])
    f_kv.start()
    f_q.start()
    w_copy = pltpu.make_async_copy(w_hbm, w_vmem, w_sem)
    w_copy.start()

    p = pos[...].reshape(1, slots)
    shift = tok.bit_length() - 1
    live = lax.broadcasted_iota(jnp.int32, (1, slots), 1) < counts[0]
    owner = jnp.where(live, lax.shift_right_logical(p, shift), -1)
    local = lax.bitwise_and(p, tok - 1).astype(f32)
    mine = owner == lax.broadcasted_iota(jnp.int32, (n, slots), 0)
    tri = lax.broadcasted_iota(jnp.int32, (slots, slots), 0) <= lax.broadcasted_iota(
        jnp.int32, (slots, slots), 1
    )
    cum = jnp.dot(mine.astype(f32).astype(bf16), tri.astype(f32).astype(bf16), preferred_element_type=f32)
    rank = jnp.sum(jnp.where(mine, cum, 0.0), axis=0, keepdims=True) - 1.0
    flat = owner.astype(f32) * float(cap) + rank
    hit = lax.broadcasted_iota(jnp.int32, (rows, slots), 0).astype(f32) == flat
    hot_s[...] = hit.astype(f32).astype(bf16)
    marks = jnp.sum(jnp.where(hit, local + 1.0, 0.0), axis=1, keepdims=True) - 1.0
    box_kv[:, 2 * ch :] = jnp.broadcast_to(marks, (rows, LANES)).astype(bf16)

    def pack_kv(c, _):
        src = pl.ds(pl.multiple_of(ch + c * tile, LANES), tile)
        dst = pl.ds(pl.multiple_of(c * tile, LANES), tile)
        box_kv[:, dst] = jnp.dot(hot_s[...], feats[:, src], preferred_element_type=f32).astype(bf16)
        return _

    def pack_q(c, _):
        dst = pl.ds(pl.multiple_of(c * tile, LANES), tile)
        box_q[:, dst] = jnp.dot(hot_s[...], feats[:, dst], preferred_element_type=f32).astype(bf16)
        return _

    f_kv.wait()
    lax.fori_loop(0, 2 * ch // tile, pack_kv, 0)

    def slab(ref, k):
        return ref.at[pl.ds(pl.multiple_of(k * cap, cap), cap), :]

    def outgoing(box, arr, send, recv, d):
        to = peer_of(d)
        return pltpu.make_async_remote_copy(
            src_ref=slab(box, to), dst_ref=slab(arr, me), send_sem=send.at[d], recv_sem=recv.at[d],
            device_id={"ctx": to}, device_id_type=MESH,
        )

    def incoming(box, arr, send, recv, d):
        came = peer_of(d)
        return pltpu.make_async_remote_copy(
            src_ref=slab(box, came), dst_ref=slab(arr, came), send_sem=send.at[d], recv_sem=recv.at[d],
            device_id={"ctx": came}, device_id_type=MESH,
        )

    def start_kv(d, c):
        outgoing(box_kv, arr_kv, send_kv, recv_kv, d).start()
        return c

    def start_q(d, c):
        outgoing(box_q, arr_q, send_q, recv_q, d).start()
        return c

    def recv_kv_wait(d, c):
        incoming(box_kv, arr_kv, send_kv, recv_kv, d).wait_recv()
        return c

    def recv_q_wait(d, c):
        incoming(box_q, arr_q, send_q, recv_q, d).wait_recv()
        return c

    def send_waits(d, c):
        outgoing(box_kv, arr_kv, send_kv, recv_kv, d).wait_send()
        outgoing(box_q, arr_q, send_q, recv_q, d).wait_send()
        return c

    pl.semaphore_wait(barrier, n - 1)
    lax.fori_loop(1, n, start_kv, 0)
    own_kv = pltpu.make_async_copy(slab(box_kv, me), slab(arr_kv, me), self_sems.at[0])
    own_kv.start()
    f_q.wait()
    lax.fori_loop(0, ch // tile, pack_q, 0)
    own_q = pltpu.make_async_copy(slab(box_q, me), slab(arr_q, me), self_sems.at[1])
    own_q.start()
    lax.fori_loop(1, 1 + up_front, start_q, 0)
    decay[...] = jnp.exp(-rate[...])

    own_kv.wait()
    lax.fori_loop(1, n, recv_kv_wait, 0)

    ext = tok + 2 * ROWS
    came_pos = jnp.transpose(arr_kv[:, 2 * ch :].astype(f32))[0:1, :]
    row = lax.broadcasted_iota(jnp.int32, (ext, 1), 0)
    want = lax.bitwise_and(row, ROWS - 1) * steps + lax.shift_right_logical(row, 3) - 2
    want = jnp.where(want < 0, -100, want).astype(f32)
    place_s[...] = (want == came_pos).astype(f32).astype(bf16)
    rim_row = lax.broadcasted_iota(jnp.int32, (16, 1), 0)
    rim_want = jnp.where(rim_row < 2, rim_row + tok - 2, -100).astype(f32)
    rim_hot = (rim_want == came_pos).astype(f32).astype(bf16)

    def rim_copy(src, dst, k, to):
        return pltpu.make_async_remote_copy(
            src_ref=src, dst_ref=dst, send_sem=rim_sems.at[2 * k], recv_sem=rim_sems.at[2 * k + 1],
            device_id={"ctx": to}, device_id_type=MESH,
        )

    after, before = lax.rem(me + 1, n), lax.rem(me + n - 1, n)

    def rim_kv_tile(c, _):
        cols = pl.ds(pl.multiple_of(c * tile, LANES), tile)
        rim_kv_out[:, cols] = jnp.dot(rim_hot, arr_kv[:, cols], preferred_element_type=f32).astype(bf16)
        return _

    def rim_q_tile(c, _):
        cols = pl.ds(pl.multiple_of(c * tile, LANES), tile)
        rim_q_out[:, cols] = jnp.dot(rim_hot, arr_q[:, cols], preferred_element_type=f32).astype(bf16)
        return _

    lax.fori_loop(0, 2 * ch // tile, rim_kv_tile, 0)
    rim_kv = rim_copy(rim_kv_out, rim_kv_in, 0, after)
    rim_kv.start()
    spans = scan_spans(n)
    cuts = [1]
    for share in PACE:
        cuts.append(min(n, cuts[-1] + share * (n - 1) // 15))
    lax.fori_loop(cuts[1], cuts[2], start_q, 0)
    rim_copy(rim_kv_out, rim_kv_in, 0, before).wait_recv()

    sub = lax.broadcasted_iota(jnp.int32, (ROWS, 1), 0)
    first = jnp.logical_and(sub == 0, me > 0)

    def featured(arr, at, w_at, rim, rim_at):
        x = jnp.dot(place_s[...], arr[:, pl.ds(pl.multiple_of(at, LANES), tile)], preferred_element_type=f32)
        w = convw[:, pl.ds(pl.multiple_of(w_at, LANES), tile)]
        y = w[0:1] * x[2 * ROWS :] + w[1:2] * x[ROWS : ROWS + tok] + w[2:3] * x[:tok]
        if rim is None:
            return y
        edge = rim[:, pl.ds(pl.multiple_of(rim_at, LANES), tile)].astype(f32)
        top = jnp.where(first, w[1:2] * edge[1:2] + w[2:3] * edge[0:1], 0.0)
        nxt = jnp.where(first, w[2:3] * edge[1:2], 0.0)
        return jnp.concatenate([y[:ROWS] + top, y[ROWS : 2 * ROWS] + nxt, y[2 * ROWS :]], axis=0)

    def product_tile(c, _):
        at = c * tile
        k = featured(arr_kv, at, ch + at, rim_kv_in, at)
        v = featured(arr_kv, ch + at, 2 * ch + at, rim_kv_in, ch + at)
        prod[:, pl.ds(pl.multiple_of(at, LANES), tile)] = k * v
        return _

    lax.fori_loop(0, ch // tile, product_tile, 0)
    lax.fori_loop(cuts[2], cuts[3], start_q, 0)

    def spread(ref, k, cols):
        return jnp.broadcast_to(ref[k : k + 1, cols], (ROWS, LANES))

    later = ((ROWS - 1 - sub) * steps).astype(f32)

    def total(terms):
        while len(terms) > 1:
            terms = [a + b for a, b in zip(terms[::2], terms[1::2])] + terms[len(terms) // 2 * 2 :]
        return terms[0]

    def local_tile(c, _):
        cols = pl.ds(pl.multiple_of(c * LANES, LANES), LANES)
        dec = [spread(decay, k, cols) for k in range(poles)]
        res = [spread(resid, k, cols) for k in range(poles)]
        gain = jnp.broadcast_to(skip[pl.ds(pl.multiple_of(c * LANES, LANES), LANES)].reshape(1, LANES), (ROWS, LANES))

        def step(i, st):
            at = pl.ds(pl.multiple_of(i * ROWS, ROWS), ROWS)
            x = prod[at, cols]
            st = tuple(d * s + x for d, s in zip(dec, st))
            filt[at, cols] = gain * x + total([r * s for r, s in zip(res, st)])
            return st

        zero = jnp.zeros((ROWS, LANES), f32)
        st = lax.fori_loop(0, steps, step, (zero,) * poles, unroll=2)
        for k in range(poles):
            state[k, :, cols] = st[k]
            fade = jnp.exp(-rate[k : k + 1, cols] * later)
            own[k : k + 1, cols] = jnp.sum(fade * st[k], axis=0, keepdims=True)
        return _

    half = ch // LANES // 2
    lax.fori_loop(0, half, local_tile, 0)
    lax.fori_loop(cuts[3], cuts[4], start_q, 0)
    lax.fori_loop(half, ch // LANES, local_tile, 0)

    def scan_copy(k, j, to):
        return pltpu.make_async_remote_copy(
            src_ref=tx.at[k], dst_ref=rx.at[3 * k + j - 1], send_sem=scan_send.at[3 * k + j - 1],
            recv_sem=scan_recv.at[3 * k + j - 1], device_id={"ctx": to}, device_id_type=MESH,
        )

    def scan_moves(k, send, act):
        span = spans[k]
        for j in range(1, 4):
            if j * span < n:
                to = me + j * span if send else me - j * span
                act(scan_copy(k, j, lax.rem(to + n, n)))

    acc[0] = jnp.zeros((poles, ch), f32)
    for k, span in enumerate(spans):
        tx[k] = own[...].astype(bf16)
        scan_moves(k, True, lambda copy: copy.start())
        stop = n if k == len(spans) - 1 or 5 + k >= len(cuts) else cuts[5 + k]
        lax.fori_loop(cuts[4 + k] if 4 + k < len(cuts) else n, stop, start_q, 0)
        scan_moves(k, False, lambda copy: copy.wait_recv())
        for j in range(1, 4):
            if j * span < n:
                got = jnp.where(me >= j * span, rx[3 * k + j - 1].astype(f32), 0.0)
                acc[0] = acc[0] + jnp.exp(-rate[...] * float(tok * (j * span - 1))) * got
                if k < len(spans) - 1:
                    own[...] = own[...] + jnp.exp(-rate[...] * float(tok * j * span)) * got

    def carry_tile(c, _):
        cols = pl.ds(pl.multiple_of(c * LANES, LANES), LANES)
        dec = [spread(decay, k, cols) for k in range(poles)]
        start = []
        for k in range(poles):
            r = rate[k : k + 1, cols]
            x = jnp.where(sub == 0, acc[0, k : k + 1, cols], pltpu.roll(state[k, :, cols], 1, 0))
            for by in (1, 2, 4):
                fade = jnp.exp(-r * float(steps * by))
                x = x + jnp.where(sub >= by, fade * pltpu.roll(x, by, 0), 0.0)
            start.append(resid[k : k + 1, cols] * x)

        def step(i, g):
            at = pl.ds(pl.multiple_of(i * ROWS, ROWS), ROWS)
            g = tuple(d * s for d, s in zip(dec, g))
            filt[at, cols] = filt[at, cols] + total(list(g))
            return g

        lax.fori_loop(0, steps, step, tuple(start), unroll=2)
        return _

    lax.fori_loop(0, ch // LANES, carry_tile, 0)

    own_q.wait()
    lax.fori_loop(1, n, recv_q_wait, 0)
    lax.fori_loop(0, ch // tile, rim_q_tile, 0)
    rim_q = rim_copy(rim_q_out, rim_q_in, 1, after)
    rim_q.start()

    def query_tile(c, _):
        at = c * tile
        prod[:, pl.ds(pl.multiple_of(at, LANES), tile)] = featured(arr_q, at, at, None, at)
        return _

    lax.fori_loop(0, ch // tile, query_tile, 0)
    rim_copy(rim_q_out, rim_q_in, 1, before).wait_recv()
    edge = rim_q_in[...].astype(f32)
    w1, w2 = convw[1:2, 0:ch], convw[2:3, 0:ch]
    prod[0:ROWS, :] = prod[0:ROWS, :] + jnp.where(first, w1 * edge[1:2] + w2 * edge[0:1], 0.0)
    prod[ROWS : 2 * ROWS, :] = prod[ROWS : 2 * ROWS, :] + jnp.where(first, w2 * edge[1:2], 0.0)

    nat = lax.broadcasted_iota(jnp.int32, (tok, 1), 0)
    seat = lax.bitwise_and(nat, steps - 1) * ROWS + lax.shift_right_logical(nat, steps.bit_length() - 1)
    order = (seat == lax.broadcasted_iota(jnp.int32, (tok, tok), 1)).astype(f32).astype(bf16)

    def gate_tile(c, _):
        cols = pl.ds(pl.multiple_of(c * tile, LANES), tile)
        rows_g = (prod[:, cols] * filt[:, cols]).astype(bf16)
        natural[:, cols] = jnp.dot(order, rows_g, preferred_element_type=f32).astype(bf16)
        return _

    lax.fori_loop(0, ch // tile, gate_tile, 0)
    w_copy.wait()

    def out_tile(c, _):
        cols = pl.ds(pl.multiple_of(c * tile, LANES), tile)
        out[:, cols] = jnp.dot(natural[...], w_vmem[:, cols], preferred_element_type=f32).astype(bf16)
        return _

    lax.fori_loop(0, ch // tile, out_tile, 0)

    lax.fori_loop(1, n, send_waits, 0)
    rim_kv.wait_send()
    rim_q.wait_send()
    for k in range(len(spans)):
        scan_moves(k, True, lambda copy: copy.wait_send())


def on_device(
    features, positions, counts, conv_weight, pole_rate, pole_residue, skip_gain, out_weight
):
    n = lax.axis_size("ctx")
    slots, feat = features.shape
    ch = feat // 3
    poles = pole_rate.shape[0]
    tok = 2 * slots // 3
    cap = 2 * tok // n
    if cap % 16 or tok & (tok - 1) or tok > 256 or conv_weight.shape[0] != 3 or ch % LANES or n & (n - 1) or n < 4:
        return plain_on_device(
            features, positions, counts, conv_weight, pole_rate, pole_residue, skip_gain, out_weight
        )
    rows = n * cap
    stages = len(scan_spans(n))
    whole = pl.BlockSpec(memory_space=pltpu.VMEM)
    dma = pltpu.SemaphoreType.DMA
    return pl.pallas_call(
        functools.partial(mega, n, cap, tok, PACE[0] * (n - 1) // 15),
        out_shape=jax.ShapeDtypeStruct((tok, ch), bf16),
        in_specs=[pl.BlockSpec(memory_space=pltpu.SMEM), pl.BlockSpec(memory_space=pl.ANY)]
        + [whole] * 5 + [pl.BlockSpec(memory_space=pl.ANY)],
        out_specs=whole,
        scratch_shapes=[
            pltpu.VMEM((rows, 2 * ch + LANES), bf16),
            pltpu.VMEM((rows, ch), bf16),
            pltpu.VMEM((rows, 2 * ch + LANES), bf16),
            pltpu.VMEM((rows, ch), bf16),
            pltpu.VMEM((rows, slots), bf16),
            pltpu.VMEM((tok + 2 * ROWS, rows), bf16),
            pltpu.VMEM((tok, ch), f32),
            pltpu.VMEM((tok, ch), f32),
            pltpu.VMEM((16, LANES), bf16),
            pltpu.VMEM((tok, ch), bf16),
            pltpu.VMEM((poles, ROWS, ch), f32),
            pltpu.VMEM((slots, feat), bf16),
            pltpu.VMEM((poles, ch), f32),
            pltpu.VMEM((16, 2 * ch), bf16),
            pltpu.VMEM((16, 2 * ch), bf16),
            pltpu.VMEM((16, ch), bf16),
            pltpu.VMEM((16, ch), bf16),
            pltpu.VMEM((poles, ch), f32),
            pltpu.VMEM((1, poles, ch), f32),
            pltpu.VMEM((stages, poles, ch), bf16),
            pltpu.VMEM((3 * stages, poles, ch), bf16),
            pltpu.VMEM(out_weight.shape, bf16),
            dma((n,)), dma((n,)), dma((n,)), dma((n,)), dma((4,)), dma((3 * stages,)), dma((3 * stages,)),
            dma((2,)), dma, dma((2,)),
        ],
        compiler_params=pltpu.CompilerParams(
            collective_id=0, has_side_effects=True, vmem_limit_bytes=60 << 20
        ),
        name="hyena",
    )(
        counts, features, positions, conv_weight, pole_rate, pole_residue,
        skip_gain, out_weight,
    )


PACE = (2, 1, 1, 2, 2)


def solution(mesh):
    return jax.shard_map(
        on_device,
        mesh=mesh,
        in_specs=(
            P(("groups", "ctx"), None),
            P(("groups", "ctx")),
            P(("groups", "ctx")),
            P(),
            P(),
            P(),
            P(),
            P(),
        ),
        out_specs=P(("groups", "ctx"), None),
        check_vma=False,
    )
```

profile of v0, /device:TPU:0, one launch (start us, length us, event | category | flops | bytes accessed | tf_op | source)
XLA Modules:
  0.0 168.9 jit_solution(9255586352682996699)
XLA Ops:
  0.7 166.1 %hyena.1 = bf16[256,1920]{1,0:T(8,128)(2,1)} custom-call(s32[1]{0:T(128)S(6)} %copy.10.counts, bf16[384,5760]{1,0:T(8,128)(2,1)} %feats_hbm.1, s32[384]{0:T(512)} %pos.1, f32[3,5760]{1,0:T(4,128)} %convw.1, f32[16,1920]{1,0:T(8,128)} %rate.1, f32[16,1920]{1,0:T(8,128)} %resid.1, f32[1920]{0:T(1024)} %skip.1, bf16[1920,1920]{1,0:T(8,128)(2,1)} %w_hbm.1), custom_call_target="tpu_custom_call" | custom-call | tf_op jit(solution)/shard_map/hyena/pallas_call | solution.py:456
  166.7 2.2 %copy.11 = bf16[256,1920]{1,0:T(8,128)(2,1)} copy(bf16[256,1920]{1,0:T(8,128)(2,1)} %hyena.1) | data formatting | bytes 1966080
where the time goes:
time: 172 us; the launch traced here: 169 us
  Pallas kernels  166 us (97%)
  local copies, waits for them, and re-layouts  2.22 us (1%)
    pallas_call x1, Pallas kernels, on_device(): pl.pallas_call(functools.partial(mega, n, cap, tok, PACE[0] * (n - 1) //...  166 us

commit v1 on v0

--- a/solution.py
+++ b/solution.py
@@ -35,8 +35,8 @@
     slot_ids = jnp.arange(slot_count, dtype=jnp.int32)
     is_live = slot_ids < counts[0]
     owners = jnp.where(is_live, positions // tok_rows, devices)
-    owner_hot = (owners[:, None] == jnp.arange(devices, dtype=jnp.int32)[None, :]).astype(jnp.int32)
-    within = jnp.sum(jnp.cumsum(owner_hot, axis=0) * owner_hot, axis=1) - 1
+    same = jnp.logical_and(owners[:, None] == owners[None, :], slot_ids[None, :] < slot_ids[:, None])
+    within = jnp.sum(same.astype(jnp.int32), axis=1)
     flat_index = jnp.where(is_live, owners * pair_cap + within, devices * pair_cap)
     outbox = (
         jnp.zeros((devices * pair_cap + 1, feat_width), features.dtype)
@@ -436,19 +436,525 @@
         scan_moves(k, True, lambda copy: copy.wait_send())
 
 
-def on_device(
-    features, positions, counts, conv_weight, pole_rate, pole_residue, skip_gain, out_weight
+def swift(
+    n, groups, cap, base, tok,
+    counts, feats_hbm, pos, convw, rate, resid, skip, w_hbm, out, most,
+    box_kv, box_q, arr_kv, arr_q, mark_out, mark_in, group_out, group_in,
+    hot_s, place_s, prod, filt, natural, state,
+    feats, decay, rim_kv_out, rim_kv_in, rim_q_out, rim_q_in, own, acc, tx, rx, w_vmem,
+    send_kv, recv_kv, send_q, recv_q, send_m, recv_m, send_g, recv_g,
+    over_send_kv, over_recv_kv, over_send_q, over_recv_q, raw,
+    rim_sems, scan_send, scan_recv, self_sems, w_sem, f_sems,
 ):
-    n = lax.axis_size("ctx")
+    me = lax.axis_index("ctx")
+    group = lax.axis_index("groups")
+    slots, feat = feats_hbm.shape
+    ch = feat // 3
+    poles = rate.shape[0]
+    steps = tok // ROWS
+    tile = col_tile(ch)
+    rows = n * cap
+    over = cap - base
+    half_n = n // 2
+    barrier = pltpu.get_barrier_semaphore()
+    bits = (n - 1).bit_length()
+
+    def flip(a, m):
+        return sum(((a // (1 << b) + m // (1 << b)) % 2) * (1 << b) for b in range(bits))
+
+    def greet(m, c):
+        pl.semaphore_signal(barrier, inc=1, device_id={"ctx": flip(me, m)}, device_id_type=MESH)
+        return c
+
+    lax.fori_loop(1, n, greet, 0)
+    for g in range(1, groups):
+        pl.semaphore_signal(barrier, inc=1, device_id={"groups": lax.rem(group + g, groups)}, device_id_type=MESH)
+    kv_cols = pl.ds(ch, 2 * ch)
+    f_kv = pltpu.make_async_copy(feats_hbm.at[:, kv_cols], feats.at[:, kv_cols], f_sems.at[0])
+    f_q = pltpu.make_async_copy(feats_hbm.at[:, pl.ds(0, ch)], feats.at[:, pl.ds(0, ch)], f_sems.at[1])
+    f_kv.start()
+    f_q.start()
+    w_copy = pltpu.make_async_copy(w_hbm, w_vmem, w_sem)
+    w_copy.start()
+
+    p = pos[...].reshape(1, slots)
+    shift = tok.bit_length() - 1
+    live = lax.broadcasted_iota(jnp.int32, (1, slots), 1) < counts[0]
+    owner = jnp.where(live, lax.shift_right_logical(p, shift), -1)
+    local = lax.bitwise_and(p, tok - 1).astype(f32)
+    mine = owner == lax.broadcasted_iota(jnp.int32, (n, slots), 0)
+    tri = lax.broadcasted_iota(jnp.int32, (slots, slots), 0) <= lax.broadcasted_iota(
+        jnp.int32, (slots, slots), 1
+    )
+    tri = tri.astype(f32).astype(bf16)
+    cum = jnp.dot(mine.astype(f32).astype(bf16), tri, preferred_element_type=f32)
+    rank = jnp.sum(jnp.where(mine, cum, 0.0), axis=0, keepdims=True) - 1.0
+    direct = jnp.logical_and(live, rank < float(base))
+    beyond = jnp.logical_and(live, rank >= float(base)).astype(f32)
+    bump = jnp.dot(jnp.broadcast_to(beyond, (16, slots)).astype(bf16), tri, preferred_element_type=f32)[0:1]
+    late = jnp.where(beyond > 0.0, bump - 1.0, -1.0)
+    apart = lax.bitwise_xor(owner, me)
+    flat = jnp.where(direct, apart.astype(f32) * float(cap) + rank, -1.0)
+    spare = jnp.where(late >= 0.0, late + float(base), -1.0)
+    hot_row = lax.broadcasted_iota(jnp.int32, (rows, slots), 0)
+    hit = jnp.logical_or(hot_row.astype(f32) == flat, lax.bitwise_and(hot_row, cap - 1).astype(f32) == spare)
+    hot_s[...] = hit.astype(f32).astype(bf16)
+
+    def pack_rows(box, first, c0):
+        def pack(c, _):
+            at = pl.ds(pl.multiple_of(first, rows // 2), rows // 2)
+            src = pl.ds(pl.multiple_of(c0 + c * tile, LANES), tile)
+            dst = pl.ds(pl.multiple_of(c * tile, LANES), tile)
+            box[at, dst] = jnp.dot(hot_s[at, :], feats[:, src], preferred_element_type=f32).astype(bf16)
+            return _
+
+        return pack
+
+    def slab(ref, k, size):
+        return ref.at[pl.ds(pl.multiple_of(k * cap, cap), size), :]
+
+    def over_rows(ref, k):
+        return ref.at[pl.ds(pl.multiple_of(k * cap + base, ROWS), over), :]
+
+    def direct_copy(which, m, size, came):
+        box, arr, send, recv = which
+        to = flip(me, m)
+        return pltpu.make_async_remote_copy(
+            src_ref=slab(box, m, size), dst_ref=slab(arr, to if came else me, size), send_sem=send.at[m],
+            recv_sem=recv.at[m], device_id={"ctx": to}, device_id_type=MESH,
+        )
+
+    def to_mirror(which, came):
+        box, arr, send, recv = which
+        to = flip(me, half_n)
+        return pltpu.make_async_remote_copy(
+            src_ref=over_rows(box, half_n), dst_ref=over_rows(arr, to if came else me), send_sem=send.at[0],
+            recv_sem=recv.at[0], device_id={"ctx": to}, device_id_type=MESH,
+        )
+
+    def forward(which, m, came):
+        box, arr, send, recv = which
+        to = flip(me, m)
+        rows_of = over_rows(arr, flip(to if came else me, half_n))
+        return pltpu.make_async_remote_copy(
+            src_ref=rows_of, dst_ref=rows_of, send_sem=send.at[m], recv_sem=recv.at[m],
+            device_id={"ctx": to}, device_id_type=MESH,
+        )
+
+    kv_direct = (box_kv, arr_kv, send_kv, recv_kv)
+    q_direct = (box_q, arr_q, send_q, recv_q)
+    kv_over = (box_kv, arr_kv, over_send_kv, over_recv_kv)
+    q_over = (box_q, arr_q, over_send_q, over_recv_q)
+
+    def each(first, last, make, act):
+        def one(m, c):
+            act(make(m))
+            return c
+
+        lax.fori_loop(first, last, one, 0)
+
+    def start(copy):
+        copy.start()
+
+    def arrive(copy):
+        copy.wait_recv()
+
+    def sent(copy):
+        copy.wait_send()
+
+    def near(which, came=False):
+        return lambda m: direct_copy(which, m, cap, came)
+
+    def far(which, came=False):
+        return lambda m: direct_copy(which, m, base, came)
+
+    def spread_over(which, came=False):
+        return lambda m: forward(which, m, came)
+
+    def marks_to(m, to, came):
+        return pltpu.make_async_remote_copy(
+            src_ref=mark_out.at[to], dst_ref=mark_in.at[came], send_sem=send_m.at[m], recv_sem=recv_m.at[m],
+            device_id={"ctx": to}, device_id_type=MESH,
+        )
+
+    def start_marks(m, c):
+        marks_to(m, flip(me, m), me).start()
+        return c
+
+    def recv_marks(m, c):
+        marks_to(m, flip(me, m), flip(me, m)).wait_recv()
+        return c
+
+    f_kv.wait()
+    lax.fori_loop(0, 2 * ch // tile, pack_rows(box_kv, rows // 2, ch), 0)
+    pl.semaphore_wait(barrier, n - 1 + groups - 1)
+    to_mirror(kv_over, False).start()
+    each(half_n, n, far(kv_direct), start)
+    lax.fori_loop(0, 2 * ch // tile, pack_rows(box_kv, 0, ch), 0)
+    each(1, half_n, near(kv_direct), start)
+    own_kv = pltpu.make_async_copy(slab(box_kv, 0, cap), slab(arr_kv, me, cap), self_sems.at[0])
+    own_kv.start()
+
+    seats = (lax.broadcasted_iota(jnp.int32, (LANES, slots), 0) - lax.rem(me * cap, LANES)).astype(f32)
+    in_slab = jnp.logical_and(seats >= 0.0, seats < float(cap))
+    at_base = jnp.logical_and(direct, seats == rank)
+    at_over = jnp.logical_and(in_slab, jnp.logical_and(late >= 0.0, seats - float(base) == late))
+    last_dims = (((1,), (1,)), ((), ()))
+    sub16 = lax.broadcasted_iota(jnp.int32, (16, slots), 0)
+    two = jnp.where(sub16 == 0, local + 1.0, jnp.where(sub16 == 1, owner.astype(f32), 0.0)).astype(bf16)
+    tell = lax.dot_general(
+        jnp.where(mine, local + 1.0, 0.0).astype(bf16), at_base.astype(f32).astype(bf16), last_dims,
+        preferred_element_type=f32,
+    )
+    tell = jnp.where(tell > 0.0, tell + (lax.broadcasted_iota(jnp.int32, (n, LANES), 0) * tok).astype(f32), 0.0)
+    extra = lax.dot_general(two, at_over.astype(f32).astype(bf16), last_dims, preferred_element_type=f32)
+    tell = tell + (extra[0:1] + extra[1:2] * float(tok))
+    held = jnp.broadcast_to(jnp.sum(beyond, axis=1, keepdims=True), (1, LANES))
+    for k in range(n):
+        mark_out[k, 0:1, :] = tell[k : k + 1, :]
+        mark_out[k, 1:2, :] = held
+    mark_in[me] = mark_out[me]
+    lax.fori_loop(1, n, start_marks, 0)
+
+    to_mirror(kv_over, True).wait_recv()
+    each(1, half_n, spread_over(kv_over), start)
+
+    f_q.wait()
+    lax.fori_loop(0, ch // tile, pack_rows(box_q, rows // 2, 0), 0)
+    to_mirror(q_over, False).start()
+    lax.fori_loop(0, ch // tile, pack_rows(box_q, 0, 0), 0)
+    own_q = pltpu.make_async_copy(slab(box_q, 0, cap), slab(arr_q, me, cap), self_sems.at[1])
+    own_q.start()
+    decay[...] = jnp.exp(-rate[...])
+
+    lax.fori_loop(1, n, recv_marks, 0)
+    lanes_of = [
+        sum(mark_in[k, 0:1, :] for k in range(g * (LANES // cap), (g + 1) * (LANES // cap)))
+        for g in range(rows // LANES)
+    ]
+    came_pos = jnp.concatenate(lanes_of, axis=1) - 1.0
+    worst = mark_in[0, 1:2, :]
+    for k in range(1, n):
+        worst = jnp.maximum(worst, mark_in[k, 1:2, :])
+    group_out[...] = jnp.broadcast_to(worst, (ROWS, LANES))
+
+    def group_copy(g, to):
+        return pltpu.make_async_remote_copy(
+            src_ref=group_out, dst_ref=group_in.at[g], send_sem=send_g.at[g], recv_sem=recv_g.at[g],
+            device_id={"groups": to}, device_id_type=MESH,
+        )
+
+    for g in range(1, groups):
+        group_copy(g, lax.rem(group + g, groups)).start()
+
+    ext = tok + 2 * ROWS
+    row = lax.broadcasted_iota(jnp.int32, (ext, 1), 0)
+    want = lax.bitwise_and(row, ROWS - 1) * steps + lax.shift_right_logical(row, 3) - 2
+    want = jnp.where(want < 0, -100, want + me * tok).astype(f32)
+    place_s[...] = (want == came_pos).astype(f32).astype(bf16)
+    rim_row = lax.broadcasted_iota(jnp.int32, (16, 1), 0)
+    rim_want = jnp.where(rim_row < 2, rim_row + me * tok + tok - 2, -100).astype(f32)
+    rim_hot = (rim_want == came_pos).astype(f32).astype(bf16)
+
+    to_mirror(q_over, True).wait_recv()
+    each(1, half_n, spread_over(q_over), start)
+    own_kv.wait()
+    each(1, half_n, near(kv_direct, True), arrive)
+    each(1, half_n, near(q_direct), start)
+    each(1, half_n, spread_over(kv_over, True), arrive)
+    cuts = [half_n]
+    for share in FLOW:
+        cuts.append(min(n, cuts[-1] + share * half_n // 8))
+    each(half_n, cuts[0] + n - cuts[1], far(kv_direct, True), arrive)
+    ahead = cuts[1] - half_n
+
+    def kv_then_q(m, c):
+        far(kv_direct, True)(m).wait_recv()
+        far(q_direct)(m - n + cuts[1]).start()
+        return c
+
+    lax.fori_loop(n - ahead, n, kv_then_q, 0)
+
+    def rim_copy(src, dst, k, to):
+        return pltpu.make_async_remote_copy(
+            src_ref=src, dst_ref=dst, send_sem=rim_sems.at[2 * k], recv_sem=rim_sems.at[2 * k + 1],
+            device_id={"ctx": to}, device_id_type=MESH,
+        )
+
+    after, before = lax.rem(me + 1, n), lax.rem(me + n - 1, n)
+
+    def rim_tile(arr, rim):
+        def fill(c, _):
+            cols = pl.ds(pl.multiple_of(c * tile, LANES), tile)
+            rim[:, cols] = jnp.dot(rim_hot, arr[:, cols], preferred_element_type=f32).astype(bf16)
+            return _
+
+        return fill
+
+    lax.fori_loop(0, 2 * ch // tile, rim_tile(arr_kv, rim_kv_out), 0)
+    rim_kv = rim_copy(rim_kv_out, rim_kv_in, 0, after)
+    rim_kv.start()
+    spans = scan_spans(n)
+
+    sub = lax.broadcasted_iota(jnp.int32, (ROWS, 1), 0)
+    first = jnp.logical_and(sub == 0, me > 0)
+
+    def featured(arr, at, w_at):
+        x = jnp.dot(place_s[...], arr[:, pl.ds(pl.multiple_of(at, LANES), tile)], preferred_element_type=f32)
+        w = convw[:, pl.ds(pl.multiple_of(w_at, LANES), tile)]
+        return w[0:1] * x[2 * ROWS :] + w[1:2] * x[ROWS : ROWS + tok] + w[2:3] * x[:tok]
+
+    def product_tile(c, _):
+        at = c * tile
+        k = featured(arr_kv, at, ch + at)
+        v = featured(arr_kv, ch + at, 2 * ch + at)
+        raw[:, pl.ds(pl.multiple_of(at, LANES), tile)] = k[: 2 * ROWS]
+        raw[:, pl.ds(pl.multiple_of(ch + at, LANES), tile)] = v[: 2 * ROWS]
+        prod[:, pl.ds(pl.multiple_of(at, LANES), tile)] = k * v
+        return _
+
+    lax.fori_loop(0, ch // tile, product_tile, 0)
+    each(cuts[1], cuts[2], far(q_direct), start)
+    rim_copy(rim_kv_out, rim_kv_in, 0, before).wait_recv()
+
+    def edge_tile(c, _):
+        def with_edge(at):
+            cols = pl.ds(pl.multiple_of(at, LANES), tile)
+            w = convw[:, pl.ds(pl.multiple_of(ch + at, LANES), tile)]
+            edge = rim_kv_in[:, cols].astype(f32)
+            top = jnp.where(first, w[1:2] * edge[1:2] + w[2:3] * edge[0:1], 0.0)
+            nxt = jnp.where(first, w[2:3] * edge[1:2], 0.0)
+            return jnp.concatenate([raw[0:ROWS, cols] + top, raw[ROWS:, cols] + nxt], axis=0)
+
+        at = c * tile
+        prod[0 : 2 * ROWS, pl.ds(pl.multiple_of(at, LANES), tile)] = with_edge(at) * with_edge(ch + at)
+        return _
+
+    lax.fori_loop(0, ch // tile, edge_tile, 0)
+
+    def spread(ref, k, cols):
+        return jnp.broadcast_to(ref[k : k + 1, cols], (ROWS, LANES))
+
+    later = ((ROWS - 1 - sub) * steps).astype(f32)
+
+    def total(terms):
+        while len(terms) > 1:
+            terms = [a + b for a, b in zip(terms[::2], terms[1::2])] + terms[len(terms) // 2 * 2 :]
+        return terms[0]
+
+    def local_tile(c, _):
+        cols = pl.ds(pl.multiple_of(c * LANES, LANES), LANES)
+        dec = [spread(decay, k, cols) for k in range(poles)]
+        res = [spread(resid, k, cols) for k in range(poles)]
+        gain = jnp.broadcast_to(skip[pl.ds(pl.multiple_of(c * LANES, LANES), LANES)].reshape(1, LANES), (ROWS, LANES))
+
+        def step(i, st):
+            at = pl.ds(pl.multiple_of(i * ROWS, ROWS), ROWS)
+            x = prod[at, cols]
+            st = tuple(d * s + x for d, s in zip(dec, st))
+            filt[at, cols] = gain * x + total([r * s for r, s in zip(res, st)])
+            return st
+
+        zero = jnp.zeros((ROWS, LANES), f32)
+        st = lax.fori_loop(0, steps, step, (zero,) * poles, unroll=2)
+        for k in range(poles):
+            state[k, :, cols] = st[k]
+            fade = jnp.exp(-rate[k : k + 1, cols] * later)
+            own[k : k + 1, cols] = jnp.sum(fade * st[k], axis=0, keepdims=True)
+        return _
+
+    middle = (ch // LANES + 1) // 2
+    parts = [(0, middle), (middle, ch // LANES)]
+
+    def scan_copy(part, k, j, to):
+        cols = pl.ds(part[0] * LANES, (part[1] - part[0]) * LANES)
+        at = (3 * k + j - 1) * len(parts) + parts.index(part)
+        return pltpu.make_async_remote_copy(
+            src_ref=tx.at[k, :, cols], dst_ref=rx.at[3 * k + j - 1, :, cols], send_sem=scan_send.at[at],
+            recv_sem=scan_recv.at[at], device_id={"ctx": to}, device_id_type=MESH,
+        )
+
+    def scan_moves(part, k, send, act):
+        span = spans[k]
+        for j in range(1, 4):
+            if j * span < n:
+                to = me + j * span if send else me - j * span
+                act(scan_copy(part, k, j, lax.rem(to + n, n)))
+
+    def scan_start(part, k):
+        cols = pl.ds(part[0] * LANES, (part[1] - part[0]) * LANES)
+        tx[k, :, cols] = own[:, cols].astype(bf16)
+        scan_moves(part, k, True, start)
+
+    def scan_take(part, k):
+        span = spans[k]
+        cols = pl.ds(part[0] * LANES, (part[1] - part[0]) * LANES)
+        scan_moves(part, k, False, arrive)
+        r = rate[:, cols]
+        for j in range(1, 4):
+            if j * span < n:
+                got = jnp.where(me >= j * span, rx[3 * k + j - 1, :, cols].astype(f32), 0.0)
+                acc[0, :, cols] = acc[0, :, cols] + jnp.exp(-r * float(tok * (j * span - 1))) * got
+                if k < len(spans) - 1:
+                    own[:, cols] = own[:, cols] + jnp.exp(-r * float(tok * j * span)) * got
+
+    acc[0] = jnp.zeros((poles, ch), f32)
+    for part in parts:
+        lax.fori_loop(part[0], part[1], local_tile, 0)
+        scan_start(part, 0)
+    each(cuts[2], cuts[3], far(q_direct), start)
+    for k in range(len(spans) - 1):
+        for part in parts:
+            scan_take(part, k)
+            scan_start(part, k + 1)
+    each(cuts[3], n, far(q_direct), start)
+
+    def carry_tile(c, _):
+        cols = pl.ds(pl.multiple_of(c * LANES, LANES), LANES)
+        dec = [spread(decay, k, cols) for k in range(poles)]
+        start = []
+        for k in range(poles):
+            r = rate[k : k + 1, cols]
+            x = jnp.where(sub == 0, acc[0, k : k + 1, cols], pltpu.roll(state[k, :, cols], 1, 0))
+            for by in (1, 2, 4):
+                fade = jnp.exp(-r * float(steps * by))
+                x = x + jnp.where(sub >= by, fade * pltpu.roll(x, by, 0), 0.0)
+            start.append(resid[k : k + 1, cols] * x)
+
+        def step(i, g):
+            at = pl.ds(pl.multiple_of(i * ROWS, ROWS), ROWS)
+            g = tuple(d * s for d, s in zip(dec, g))
+            filt[at, cols] = filt[at, cols] + total(list(g))
+            return g
+
+        lax.fori_loop(0, steps, step, tuple(start), unroll=2)
+        return _
+
+    for part in parts:
+        scan_take(part, len(spans) - 1)
+        lax.fori_loop(part[0], part[1], carry_tile, 0)
+    top_of = worst
+    for g in range(1, groups):
+        group_copy(g, lax.rem(group + groups - g, groups)).wait_recv()
+        top_of = jnp.maximum(top_of, group_in[g, 0:1, :])
+    most[...] = jnp.broadcast_to(top_of, (ROWS, LANES))
+    w_copy.wait()
+
+    own_q.wait()
+    each(1, half_n, near(q_direct, True), arrive)
+    each(1, half_n, spread_over(q_over, True), arrive)
+    each(half_n, n, far(q_direct, True), arrive)
+    lax.fori_loop(0, ch // tile, rim_tile(arr_q, rim_q_out), 0)
+    rim_q = rim_copy(rim_q_out, rim_q_in, 1, after)
+    rim_q.start()
+
+    def query_tile(c, _):
+        at = c * tile
+        prod[:, pl.ds(pl.multiple_of(at, LANES), tile)] = featured(arr_q, at, at)
+        return _
+
+    lax.fori_loop(0, ch // tile, query_tile, 0)
+    rim_copy(rim_q_out, rim_q_in, 1, before).wait_recv()
+    edge = rim_q_in[...].astype(f32)
+    w1, w2 = convw[1:2, 0:ch], convw[2:3, 0:ch]
+    prod[0:ROWS, :] = prod[0:ROWS, :] + jnp.where(first, w1 * edge[1:2] + w2 * edge[0:1], 0.0)
+    prod[ROWS : 2 * ROWS, :] = prod[ROWS : 2 * ROWS, :] + jnp.where(first, w2 * edge[1:2], 0.0)
+
+    nat = lax.broadcasted_iota(jnp.int32, (tok, 1), 0)
+    seat = lax.bitwise_and(nat, steps - 1) * ROWS + lax.shift_right_logical(nat, steps.bit_length() - 1)
+    order = (seat == lax.broadcasted_iota(jnp.int32, (tok, tok), 1)).astype(f32).astype(bf16)
+
+    def gate_tile(c, _):
+        cols = pl.ds(pl.multiple_of(c * tile, LANES), tile)
+        rows_g = (prod[:, cols] * filt[:, cols]).astype(bf16)
+        natural[:, cols] = jnp.dot(order, rows_g, preferred_element_type=f32).astype(bf16)
+        return _
+
+    lax.fori_loop(0, ch // tile, gate_tile, 0)
+
+    def out_tile(c, _):
+        cols = pl.ds(pl.multiple_of(c * tile, LANES), tile)
+        out[:, cols] = jnp.dot(natural[...], w_vmem[:, cols], preferred_element_type=f32).astype(bf16)
+        return _
+
+    lax.fori_loop(0, ch // tile, out_tile, 0)
+
+    for which in (kv_direct, q_direct):
+        each(1, half_n, near(which), sent)
+        each(half_n, n, far(which), sent)
+    for which in (kv_over, q_over):
+        to_mirror(which, False).wait_send()
+        each(1, half_n, spread_over(which), sent)
+    each(1, n, lambda m: marks_to(m, flip(me, m), me), sent)
+    for g in range(1, groups):
+        group_copy(g, lax.rem(group + g, groups)).wait_send()
+    rim_kv.wait_send()
+    rim_q.wait_send()
+    for k in range(len(spans)):
+        for part in parts:
+            scan_moves(part, k, True, sent)
+
+
+def swift_call(n, groups, cap, base, tok, args):
+    counts, features, positions, conv_weight, pole_rate, pole_residue, skip_gain, out_weight = args
     slots, feat = features.shape
     ch = feat // 3
     poles = pole_rate.shape[0]
-    tok = 2 * slots // 3
-    cap = 2 * tok // n
-    if cap % 16 or tok & (tok - 1) or tok > 256 or conv_weight.shape[0] != 3 or ch % LANES or n & (n - 1) or n < 4:
-        return plain_on_device(
-            features, positions, counts, conv_weight, pole_rate, pole_residue, skip_gain, out_weight
-        )
+    rows = n * cap
+    stages = len(scan_spans(n))
+    whole = pl.BlockSpec(memory_space=pltpu.VMEM)
+    dma = pltpu.SemaphoreType.DMA
+    vmem = pltpu.VMEM
+    return pl.pallas_call(
+        functools.partial(swift, n, groups, cap, base, tok),
+        out_shape=(jax.ShapeDtypeStruct((tok, ch), bf16), jax.ShapeDtypeStruct((ROWS, LANES), f32)),
+        in_specs=[pl.BlockSpec(memory_space=pltpu.SMEM), pl.BlockSpec(memory_space=pl.ANY)]
+        + [whole] * 5 + [pl.BlockSpec(memory_space=pl.ANY)],
+        out_specs=(whole, whole),
+        scratch_shapes=[
+            vmem((rows, 2 * ch), bf16),
+            vmem((rows, ch), bf16),
+            vmem((rows, 2 * ch), bf16),
+            vmem((rows, ch), bf16),
+            vmem((n, 2, LANES), f32),
+            vmem((n, 2, LANES), f32),
+            vmem((ROWS, LANES), f32),
+            vmem((groups, ROWS, LANES), f32),
+            vmem((rows, slots), bf16),
+            vmem((tok + 2 * ROWS, rows), bf16),
+            vmem((tok, ch), f32),
+            vmem((tok, ch), f32),
+            vmem((tok, ch), bf16),
+            vmem((poles, ROWS, ch), f32),
+            vmem((slots, feat), bf16),
+            vmem((poles, ch), f32),
+            vmem((16, 2 * ch), bf16),
+            vmem((16, 2 * ch), bf16),
+            vmem((16, ch), bf16),
+            vmem((16, ch), bf16),
+            vmem((poles, ch), f32),
+            vmem((1, poles, ch), f32),
+            vmem((stages, poles, ch), bf16),
+            vmem((3 * stages, poles, ch), bf16),
+            vmem(out_weight.shape, bf16),
+        ]
+        + [dma((n,))] * 6
+        + [dma((groups,))] * 2
+        + [dma((n,))] * 4
+        + [vmem((2 * ROWS, 2 * ch), f32)]
+        + [dma((4,)), dma((6 * stages,)), dma((6 * stages,)), dma((2,)), dma, dma((2,))],
+        compiler_params=pltpu.CompilerParams(
+            collective_id=1, has_side_effects=True, vmem_limit_bytes=60 << 20
+        ),
+        name="hyena_direct",
+    )(*args)
+
+
+def mega_call(n, cap, tok, args):
+    counts, features, positions, conv_weight, pole_rate, pole_residue, skip_gain, out_weight = args
+    slots, feat = features.shape
+    ch = feat // 3
+    poles = pole_rate.shape[0]
     rows = n * cap
     stages = len(scan_spans(n))
     whole = pl.BlockSpec(memory_space=pltpu.VMEM)
@@ -489,13 +995,32 @@
             collective_id=0, has_side_effects=True, vmem_limit_bytes=60 << 20
         ),
         name="hyena",
-    )(
-        counts, features, positions, conv_weight, pole_rate, pole_residue,
-        skip_gain, out_weight,
-    )
+    )(*args)
+
+
+def on_device(
+    features, positions, counts, conv_weight, pole_rate, pole_residue, skip_gain, out_weight
+):
+    n = lax.axis_size("ctx")
+    groups = lax.axis_size("groups")
+    slots, feat = features.shape
+    ch = feat // 3
+    tok = 2 * slots // 3
+    cap = 2 * tok // n
+    if cap % 16 or tok & (tok - 1) or tok > 256 or conv_weight.shape[0] != 3 or ch % LANES or n & (n - 1) or n < 4:
+        return plain_on_device(
+            features, positions, counts, conv_weight, pole_rate, pole_residue, skip_gain, out_weight
+        )
+    args = (counts, features, positions, conv_weight, pole_rate, pole_residue, skip_gain, out_weight)
+    base = slots // n
+    if base % ROWS or cap - base > 16 or LANES % cap:
+        return mega_call(n, cap, tok, args)
+    done, most = swift_call(n, groups, cap, base, tok, args)
+    return lax.cond(most[0, 0] > float(cap - base), lambda d: mega_call(n, cap, tok, args), lambda d: d, done)
 
 
 PACE = (2, 1, 1, 2, 2)
+FLOW = (3, 1, 2)
 
 
 def solution(mesh):

time: 172 us -> 141 us (0.82); the launches traced: 169 us -> 140 us
  Pallas kernels: 166 us -> 137 us
    pallas_call x1, Pallas kernels: 166 us -> 137 us  [swift_call(): pl.pallas_call(functools.partial(swift, n, groups, cap, base, tok), out_s...]
where the time goes in v1:
time: 141 us; the launch traced here: 140 us
  Pallas kernels  137 us (97%)
  local copies, waits for them, and re-layouts  2.15 us (2%)
  between operations  1.41 us (1%)
    pallas_call x1, Pallas kernels, swift_call(): pl.pallas_call(functools.partial(swift, n, groups, cap, base, tok), out_s...  137 us

profile of v1, /device:TPU:0, one launch (start us, length us, event | category | flops | bytes accessed | tf_op | source)
XLA Modules:
  0.0 140.4 jit_solution(5778630310806103477)
XLA Ops:
  0.0 0.0 copy-start.3
  0.0 0.0 copy-start.1
  0.0 0.0 copy-start
  0.0 0.0 copy-start.2
  0.0 0.0 copy-start.4
  0.7 136.8 %hyena_direct.1 = (bf16[256,1920]{1,0:T(8,128)(2,1)S(1)}, f32[8,128]{1,0:T(8,128)}) custom-call(s32[1]{0:T(128)S(6)} %copy.14.counts, bf16[384,5760]{1,0:T(8,128)(2,1)} %feats_hbm.1, s32[384]{0:T(512)} %pos.1, f32[3,5760]{1,0:T(4,128)} %convw.1, f32[16,1920]{1,0:T(8,128)} %rate.1, f32[16,1920]{1,0:T(8,128)} %resid.1, f32[1920]{0:T(1024)} %skip.1, ...), custom_call_target="tpu_custom_call" | custom-call | tf_op jit(solution)/shard_map/hyena_direct/pallas_call | solution.py:908
  137.5 1.2 slice.3
  139.4 0.0 copy-done.3
  139.4 0.0 copy-done.1
  139.4 0.0 copy-done
  139.4 0.0 copy-done.2
  139.4 0.0 copy-done.4
  139.4 0.9 copy.15
  (1 shorter events, 0.0 us)
Async XLA Ops:
  0.0 139.4 %copy-start.3 = (f32[1920]{0:T(1024)S(1)}, f32[1920]{0:T(1024)}, u32[]{:S(2)}) copy-start(f32[1920]{0:T(1024)} %skip.1) | copy-start | bytes 23044
  0.0 139.4 %copy-start.1 = (f32[16,1920]{1,0:T(8,128)S(1)}, f32[16,1920]{1,0:T(8,128)}, u32[]{:S(2)}) copy-start(f32[16,1920]{1,0:T(8,128)} %resid.1) | copy-start | bytes 368644
  0.0 139.4 %copy-start = (f32[16,1920]{1,0:T(8,128)S(1)}, f32[16,1920]{1,0:T(8,128)}, u32[]{:S(2)}) copy-start(f32[16,1920]{1,0:T(8,128)} %rate.1) | copy-start | bytes 368644
  0.0 139.4 %copy-start.2 = (f32[3,5760]{1,0:T(4,128)S(1)}, f32[3,5760]{1,0:T(4,128)}, u32[]{:S(2)}) copy-start(f32[3,5760]{1,0:T(4,128)} %convw.1) | copy-start | bytes 207364
  0.0 139.4 %copy-start.4 = (s32[384]{0:T(512)S(1)}, s32[384]{0:T(512)}, u32[]{:S(2)}) copy-start(s32[384]{0:T(512)} %pos.1) | copy-start | bytes 4612

commit v2 on v1

--- a/solution.py
+++ b/solution.py
@@ -440,10 +440,10 @@
     n, groups, cap, base, tok,
     counts, feats_hbm, pos, convw, rate, resid, skip, w_hbm, out, most,
     box_kv, box_q, arr_kv, arr_q, mark_out, mark_in, group_out, group_in,
-    hot_s, place_s, prod, filt, natural, state,
+    hot_s, place_s, prod, filt, gated, natural, state,
     feats, decay, rim_kv_out, rim_kv_in, rim_q_out, rim_q_in, own, acc, tx, rx, w_vmem,
     send_kv, recv_kv, send_q, recv_q, send_m, recv_m, send_g, recv_g,
-    over_send_kv, over_recv_kv, over_send_q, over_recv_q, raw,
+    over_send_kv, over_recv_kv, over_send_q, over_recv_q, raw, ending, inward, hops, leaps,
     rim_sems, scan_send, scan_recv, self_sems, w_sem, f_sems,
 ):
     me = lax.axis_index("ctx")
@@ -626,6 +626,29 @@
     own_q = pltpu.make_async_copy(slab(box_q, 0, cap), slab(arr_q, me, cap), self_sems.at[1])
     own_q.start()
     decay[...] = jnp.exp(-rate[...])
+    spans = scan_spans(n)
+    sub = lax.broadcasted_iota(jnp.int32, (ROWS, 1), 0)
+    first = jnp.logical_and(sub == 0, me > 0)
+    later = ((ROWS - 1 - sub) * steps).astype(f32)
+    segment = (sub * steps).astype(f32)
+    leap_of = {}
+    for k, span in enumerate(spans):
+        for j in range(1, 4):
+            if j * span < n:
+                for lag in (j * span - 1,) + ((j * span,) if k < len(spans) - 1 else ()):
+                    leap_of.setdefault(lag, len(leap_of))
+    for lag, at in leap_of.items():
+        leaps[at] = jnp.exp(-rate[...] * float(tok * lag))
+    for at, by in enumerate((1, 2, 4)):
+        hops[at] = jnp.exp(-rate[...] * float(steps * by))
+
+    def fades_of(k, _):
+        r = rate[pl.ds(k, 1), :]
+        ending[k] = jnp.exp(-r * later)
+        inward[k] = resid[pl.ds(k, 1), :] * jnp.exp(-r * segment)
+        return _
+
+    lax.fori_loop(0, poles, fades_of, 0)
 
     lax.fori_loop(1, n, recv_marks, 0)
     lanes_of = [
@@ -694,10 +717,6 @@
     lax.fori_loop(0, 2 * ch // tile, rim_tile(arr_kv, rim_kv_out), 0)
     rim_kv = rim_copy(rim_kv_out, rim_kv_in, 0, after)
     rim_kv.start()
-    spans = scan_spans(n)
-
-    sub = lax.broadcasted_iota(jnp.int32, (ROWS, 1), 0)
-    first = jnp.logical_and(sub == 0, me > 0)
 
     def featured(arr, at, w_at):
         x = jnp.dot(place_s[...], arr[:, pl.ds(pl.multiple_of(at, LANES), tile)], preferred_element_type=f32)
@@ -735,8 +754,6 @@
     def spread(ref, k, cols):
         return jnp.broadcast_to(ref[k : k + 1, cols], (ROWS, LANES))
 
-    later = ((ROWS - 1 - sub) * steps).astype(f32)
-
     def total(terms):
         while len(terms) > 1:
             terms = [a + b for a, b in zip(terms[::2], terms[1::2])] + terms[len(terms) // 2 * 2 :]
@@ -756,11 +773,19 @@
             return st
 
         zero = jnp.zeros((ROWS, LANES), f32)
-        st = lax.fori_loop(0, steps, step, (zero,) * poles, unroll=2)
+        st = lax.fori_loop(0, steps, step, (zero,) * poles, unroll=4)
         for k in range(poles):
             state[k, :, cols] = st[k]
-            fade = jnp.exp(-rate[k : k + 1, cols] * later)
-            own[k : k + 1, cols] = jnp.sum(fade * st[k], axis=0, keepdims=True)
+            own[k : k + 1, cols] = jnp.sum(ending[k, :, cols] * st[k], axis=0, keepdims=True)
+        return _
+
+    def prefix_tile(c, _):
+        cols = pl.ds(pl.multiple_of(c * LANES, LANES), LANES)
+        for k in range(poles):
+            x = jnp.where(sub == 0, 0.0, pltpu.roll(state[k, :, cols], 1, 0))
+            for at, by in enumerate((1, 2, 4)):
+                x = x + jnp.where(sub >= by, hops[at, k : k + 1, cols] * pltpu.roll(x, by, 0), 0.0)
+            state[k, :, cols] = resid[k : k + 1, cols] * x
         return _
 
     middle = (ch // LANES + 1) // 2
@@ -790,19 +815,19 @@
         span = spans[k]
         cols = pl.ds(part[0] * LANES, (part[1] - part[0]) * LANES)
         scan_moves(part, k, False, arrive)
-        r = rate[:, cols]
         for j in range(1, 4):
             if j * span < n:
                 got = jnp.where(me >= j * span, rx[3 * k + j - 1, :, cols].astype(f32), 0.0)
-                acc[0, :, cols] = acc[0, :, cols] + jnp.exp(-r * float(tok * (j * span - 1))) * got
+                acc[0, :, cols] = acc[0, :, cols] + leaps[leap_of[j * span - 1], :, cols] * got
                 if k < len(spans) - 1:
-                    own[:, cols] = own[:, cols] + jnp.exp(-r * float(tok * j * span)) * got
+                    own[:, cols] = own[:, cols] + leaps[leap_of[j * span], :, cols] * got
 
     acc[0] = jnp.zeros((poles, ch), f32)
     for part in parts:
         lax.fori_loop(part[0], part[1], local_tile, 0)
         scan_start(part, 0)
     each(cuts[2], cuts[3], far(q_direct), start)
+    lax.fori_loop(0, ch // LANES, prefix_tile, 0)
     for k in range(len(spans) - 1):
         for part in parts:
             scan_take(part, k)
@@ -812,14 +837,9 @@
     def carry_tile(c, _):
         cols = pl.ds(pl.multiple_of(c * LANES, LANES), LANES)
         dec = [spread(decay, k, cols) for k in range(poles)]
-        start = []
-        for k in range(poles):
-            r = rate[k : k + 1, cols]
-            x = jnp.where(sub == 0, acc[0, k : k + 1, cols], pltpu.roll(state[k, :, cols], 1, 0))
-            for by in (1, 2, 4):
-                fade = jnp.exp(-r * float(steps * by))
-                x = x + jnp.where(sub >= by, fade * pltpu.roll(x, by, 0), 0.0)
-            start.append(resid[k : k + 1, cols] * x)
+        begin = tuple(
+            state[k, :, cols] + inward[k, :, cols] * acc[0, k : k + 1, cols] for k in range(poles)
+        )
 
         def step(i, g):
             at = pl.ds(pl.multiple_of(i * ROWS, ROWS), ROWS)
@@ -827,7 +847,7 @@
             filt[at, cols] = filt[at, cols] + total(list(g))
             return g
 
-        lax.fori_loop(0, steps, step, tuple(start), unroll=2)
+        lax.fori_loop(0, steps, step, begin, unroll=4)
         return _
 
     for part in parts:
@@ -837,7 +857,7 @@
     for g in range(1, groups):
         group_copy(g, lax.rem(group + groups - g, groups)).wait_recv()
         top_of = jnp.maximum(top_of, group_in[g, 0:1, :])
-    most[...] = jnp.broadcast_to(top_of, (ROWS, LANES))
+    most[0] = jnp.max(top_of).astype(jnp.int32)
     w_copy.wait()
 
     own_q.wait()
@@ -848,29 +868,33 @@
     rim_q = rim_copy(rim_q_out, rim_q_in, 1, after)
     rim_q.start()
 
-    def query_tile(c, _):
+    def gate_tile(c, _):
         at = c * tile
-        prod[:, pl.ds(pl.multiple_of(at, LANES), tile)] = featured(arr_q, at, at)
-        return _
-
-    lax.fori_loop(0, ch // tile, query_tile, 0)
+        cols = pl.ds(pl.multiple_of(at, LANES), tile)
+        y = featured(arr_q, at, at)
+        raw[:, cols] = y[: 2 * ROWS]
+        gated[:, cols] = (y * filt[:, cols]).astype(bf16)
+        return _
+
+    lax.fori_loop(0, ch // tile, gate_tile, 0)
     rim_copy(rim_q_out, rim_q_in, 1, before).wait_recv()
     edge = rim_q_in[...].astype(f32)
     w1, w2 = convw[1:2, 0:ch], convw[2:3, 0:ch]
-    prod[0:ROWS, :] = prod[0:ROWS, :] + jnp.where(first, w1 * edge[1:2] + w2 * edge[0:1], 0.0)
-    prod[ROWS : 2 * ROWS, :] = prod[ROWS : 2 * ROWS, :] + jnp.where(first, w2 * edge[1:2], 0.0)
+    top = jnp.where(first, w1 * edge[1:2] + w2 * edge[0:1], 0.0)
+    nxt = jnp.where(first, w2 * edge[1:2], 0.0)
+    begun = raw[:, 0:ch] + jnp.concatenate([top, nxt], axis=0)
+    gated[0 : 2 * ROWS, :] = (begun * filt[0 : 2 * ROWS, :]).astype(bf16)
 
     nat = lax.broadcasted_iota(jnp.int32, (tok, 1), 0)
     seat = lax.bitwise_and(nat, steps - 1) * ROWS + lax.shift_right_logical(nat, steps.bit_length() - 1)
     order = (seat == lax.broadcasted_iota(jnp.int32, (tok, tok), 1)).astype(f32).astype(bf16)
 
-    def gate_tile(c, _):
+    def order_tile(c, _):
         cols = pl.ds(pl.multiple_of(c * tile, LANES), tile)
-        rows_g = (prod[:, cols] * filt[:, cols]).astype(bf16)
-        natural[:, cols] = jnp.dot(order, rows_g, preferred_element_type=f32).astype(bf16)
-        return _
-
-    lax.fori_loop(0, ch // tile, gate_tile, 0)
+        natural[:, cols] = jnp.dot(order, gated[:, cols], preferred_element_type=f32).astype(bf16)
+        return _
+
+    lax.fori_loop(0, ch // tile, order_tile, 0)
 
     def out_tile(c, _):
         cols = pl.ds(pl.multiple_of(c * tile, LANES), tile)
@@ -907,10 +931,10 @@
     vmem = pltpu.VMEM
     return pl.pallas_call(
         functools.partial(swift, n, groups, cap, base, tok),
-        out_shape=(jax.ShapeDtypeStruct((tok, ch), bf16), jax.ShapeDtypeStruct((ROWS, LANES), f32)),
+        out_shape=(jax.ShapeDtypeStruct((tok, ch), bf16), jax.ShapeDtypeStruct((1,), jnp.int32)),
         in_specs=[pl.BlockSpec(memory_space=pltpu.SMEM), pl.BlockSpec(memory_space=pl.ANY)]
         + [whole] * 5 + [pl.BlockSpec(memory_space=pl.ANY)],
-        out_specs=(whole, whole),
+        out_specs=(whole, pl.BlockSpec(memory_space=pltpu.SMEM)),
         scratch_shapes=[
             vmem((rows, 2 * ch), bf16),
             vmem((rows, ch), bf16),
@@ -924,6 +948,7 @@
             vmem((tok + 2 * ROWS, rows), bf16),
             vmem((tok, ch), f32),
             vmem((tok, ch), f32),
+            vmem((tok, ch), bf16),
             vmem((tok, ch), bf16),
             vmem((poles, ROWS, ch), f32),
             vmem((slots, feat), bf16),
@@ -941,7 +966,13 @@
         + [dma((n,))] * 6
         + [dma((groups,))] * 2
         + [dma((n,))] * 4
-        + [vmem((2 * ROWS, 2 * ch), f32)]
+        + [
+            vmem((2 * ROWS, 2 * ch), f32),
+            vmem((poles, ROWS, ch), f32),
+            vmem((poles, ROWS, ch), f32),
+            vmem((3, poles, ch), f32),
+            vmem((6 * stages, poles, ch), f32),
+        ]
         + [dma((4,)), dma((6 * stages,)), dma((6 * stages,)), dma((2,)), dma, dma((2,))],
         compiler_params=pltpu.CompilerParams(
             collective_id=1, has_side_effects=True, vmem_limit_bytes=60 << 20
@@ -1016,11 +1047,11 @@
     if base % ROWS or cap - base > 16 or LANES % cap:
         return mega_call(n, cap, tok, args)
     done, most = swift_call(n, groups, cap, base, tok, args)
-    return lax.cond(most[0, 0] > float(cap - base), lambda d: mega_call(n, cap, tok, args), lambda d: d, done)
+    return lax.cond(most[0] > cap - base, lambda d: mega_call(n, cap, tok, args), lambda d: d, done)
 
 
 PACE = (2, 1, 1, 2, 2)
-FLOW = (3, 1, 2)
+FLOW = (4, 2, 1)
 
 
 def solution(mesh):

time: 141 us -> 137 us (0.972)
  Pallas kernels: 137 us -> 134 us
    pallas_call x1, Pallas kernels: 137 us -> 134 us  [swift_call(): pl.pallas_call(functools.partial(swift, n, groups, cap, base, tok), out_s...]
where the time goes in v2:
time: 137 us
  Pallas kernels  134 us (98%)
    pallas_call x1, Pallas kernels, swift_call(): pl.pallas_call(functools.partial(swift, n, groups, cap, base, tok), out_s...  134 us

profile of v2, /device:TPU:0, one launch (start us, length us, event | category | flops | bytes accessed | tf_op | source)
XLA Modules:
  0.0 136.7 jit_solution(9581820351619369833)
XLA Ops:
  0.0 0.0 copy-start.3
  0.0 0.0 copy-start.1
  0.0 0.0 copy-start
  0.0 0.0 copy-start.2
  0.0 0.0 copy-start.4
  0.7 134.4 %hyena_direct.1 = (bf16[256,1920]{1,0:T(8,128)(2,1)S(1)}, s32[1]{0:T(128)}) custom-call(s32[1]{0:T(128)S(6)} %copy.14.counts, bf16[384,5760]{1,0:T(8,128)(2,1)} %feats_hbm.1, s32[384]{0:T(512)} %pos.1, f32[3,5760]{1,0:T(4,128)} %convw.1, f32[16,1920]{1,0:T(8,128)} %rate.1, f32[16,1920]{1,0:T(8,128)} %resid.1, f32[1920]{0:T(1024)} %skip.1, ...), custom_call_target="tpu_custom_call" | custom-call | tf_op jit(solution)/shard_map/hyena_direct/pallas_call | solution.py:932
  135.7 0.0 copy-done.3
  135.7 0.0 copy-done.1
  135.7 0.0 copy-done
  135.7 0.0 copy-done.2
  135.7 0.0 copy-done.4
  135.7 0.9 copy.15
  (1 shorter events, 0.0 us)
Async XLA Ops:
  0.0 135.7 %copy-start.3 = (f32[1920]{0:T(1024)S(1)}, f32[1920]{0:T(1024)}, u32[]{:S(2)}) copy-start(f32[1920]{0:T(1024)} %skip.1) | copy-start | bytes 23044
  0.0 135.7 %copy-start.1 = (f32[16,1920]{1,0:T(8,128)S(1)}, f32[16,1920]{1,0:T(8,128)}, u32[]{:S(2)}) copy-start(f32[16,1920]{1,0:T(8,128)} %resid.1) | copy-start | bytes 368644
  0.0 135.7 %copy-start = (f32[16,1920]{1,0:T(8,128)S(1)}, f32[16,1920]{1,0:T(8,128)}, u32[]{:S(2)}) copy-start(f32[16,1920]{1,0:T(8,128)} %rate.1) | copy-start | bytes 368644
  0.0 135.7 %copy-start.2 = (f32[3,5760]{1,0:T(4,128)S(1)}, f32[3,5760]{1,0:T(4,128)}, u32[]{:S(2)}) copy-start(f32[3,5760]{1,0:T(4,128)} %convw.1) | copy-start | bytes 207364
  0.0 135.7 %copy-start.4 = (s32[384]{0:T(512)S(1)}, s32[384]{0:T(512)}, u32[]{:S(2)}) copy-start(s32[384]{0:T(512)} %pos.1) | copy-start | bytes 4612

commit v3 on v2

--- a/solution.py
+++ b/solution.py
@@ -439,11 +439,10 @@
 def swift(
     n, groups, cap, base, tok,
     counts, feats_hbm, pos, convw, rate, resid, skip, w_hbm, out, most,
-    box_kv, box_q, arr_kv, arr_q, mark_out, mark_in, group_out, group_in,
+    box_a, box_b, box_q, arr_a, arr_b, arr_q, mark_out, mark_in, group_out, group_in,
     hot_s, place_s, prod, filt, gated, natural, state,
-    feats, decay, rim_kv_out, rim_kv_in, rim_q_out, rim_q_in, own, acc, tx, rx, w_vmem,
-    send_kv, recv_kv, send_q, recv_q, send_m, recv_m, send_g, recv_g,
-    over_send_kv, over_recv_kv, over_send_q, over_recv_q, raw, ending, inward, hops, leaps,
+    feats, decay, rims_out, rims_in, own, acc, totals, rate4, tx, rx, w_vmem,
+    sends, recvs, over_sends, over_recvs, send_m, recv_m, send_g, recv_g, raw, ending, inward, hops, leaps,
     rim_sems, scan_send, scan_recv, self_sems, w_sem, f_sems,
 ):
     me = lax.axis_index("ctx")
@@ -456,6 +455,9 @@
     rows = n * cap
     over = cap - base
     half_n = n // 2
+    tiles = ch // tile
+    lead = (tiles + 1) // 2
+    parts = [(0, lead), (lead, tiles)]
     barrier = pltpu.get_barrier_semaphore()
     bits = (n - 1).bit_length()
 
@@ -500,15 +502,23 @@
     hit = jnp.logical_or(hot_row.astype(f32) == flat, lax.bitwise_and(hot_row, cap - 1).astype(f32) == spare)
     hot_s[...] = hit.astype(f32).astype(bf16)
 
-    def pack_rows(box, first, c0):
+    def pack_rows(box, first, count, source):
         def pack(c, _):
-            at = pl.ds(pl.multiple_of(first, rows // 2), rows // 2)
-            src = pl.ds(pl.multiple_of(c0 + c * tile, LANES), tile)
+            at = pl.ds(first, rows // 2)
+            src = pl.ds(pl.multiple_of(source(c), LANES), tile)
             dst = pl.ds(pl.multiple_of(c * tile, LANES), tile)
             box[at, dst] = jnp.dot(hot_s[at, :], feats[:, src], preferred_element_type=f32).astype(bf16)
             return _
 
-        return pack
+        lax.fori_loop(0, count, pack, 0)
+
+    def pack_kv(i, first):
+        t0, t1 = parts[i]
+        count = t1 - t0
+        pack_rows(boxes[i], first, 2 * count, lambda c: ch + (c // count) * ch + (t0 + c % count) * tile)
+
+    boxes = (box_a, box_b, box_q)
+    arrs = (arr_a, arr_b, arr_q)
 
     def slab(ref, k, size):
         return ref.at[pl.ds(pl.multiple_of(k * cap, cap), size), :]
@@ -517,7 +527,7 @@
         return ref.at[pl.ds(pl.multiple_of(k * cap + base, ROWS), over), :]
 
     def direct_copy(which, m, size, came):
-        box, arr, send, recv = which
+        box, arr, send, recv = boxes[which], arrs[which], sends.at[which], recvs.at[which]
         to = flip(me, m)
         return pltpu.make_async_remote_copy(
             src_ref=slab(box, m, size), dst_ref=slab(arr, to if came else me, size), send_sem=send.at[m],
@@ -525,7 +535,7 @@
         )
 
     def to_mirror(which, came):
-        box, arr, send, recv = which
+        box, arr, send, recv = boxes[which], arrs[which], over_sends.at[which], over_recvs.at[which]
         to = flip(me, half_n)
         return pltpu.make_async_remote_copy(
             src_ref=over_rows(box, half_n), dst_ref=over_rows(arr, to if came else me), send_sem=send.at[0],
@@ -533,7 +543,7 @@
         )
 
     def forward(which, m, came):
-        box, arr, send, recv = which
+        arr, send, recv = arrs[which], over_sends.at[which], over_recvs.at[which]
         to = flip(me, m)
         rows_of = over_rows(arr, flip(to if came else me, half_n))
         return pltpu.make_async_remote_copy(
@@ -541,10 +551,7 @@
             device_id={"ctx": to}, device_id_type=MESH,
         )
 
-    kv_direct = (box_kv, arr_kv, send_kv, recv_kv)
-    q_direct = (box_q, arr_q, send_q, recv_q)
-    kv_over = (box_kv, arr_kv, over_send_kv, over_recv_kv)
-    q_over = (box_q, arr_q, over_send_q, over_recv_q)
+    in_a, in_b, in_q = 0, 1, 2
 
     def each(first, last, make, act):
         def one(m, c):
@@ -585,15 +592,17 @@
         marks_to(m, flip(me, m), flip(me, m)).wait_recv()
         return c
 
+    def own_copy(i):
+        return pltpu.make_async_copy(slab(boxes[i], 0, cap), slab(arrs[i], me, cap), self_sems.at[i])
+
     f_kv.wait()
-    lax.fori_loop(0, 2 * ch // tile, pack_rows(box_kv, rows // 2, ch), 0)
+    pack_kv(in_a, rows // 2)
     pl.semaphore_wait(barrier, n - 1 + groups - 1)
-    to_mirror(kv_over, False).start()
-    each(half_n, n, far(kv_direct), start)
-    lax.fori_loop(0, 2 * ch // tile, pack_rows(box_kv, 0, ch), 0)
-    each(1, half_n, near(kv_direct), start)
-    own_kv = pltpu.make_async_copy(slab(box_kv, 0, cap), slab(arr_kv, me, cap), self_sems.at[0])
-    own_kv.start()
+    to_mirror(in_a, False).start()
+    each(half_n, n, far(in_a), start)
+    pack_kv(in_a, 0)
+    each(1, half_n, near(in_a), start)
+    own_copy(in_a).start()
 
     seats = (lax.broadcasted_iota(jnp.int32, (LANES, slots), 0) - lax.rem(me * cap, LANES)).astype(f32)
     in_slab = jnp.logical_and(seats >= 0.0, seats < float(cap))
@@ -616,29 +625,37 @@
     mark_in[me] = mark_out[me]
     lax.fori_loop(1, n, start_marks, 0)
 
-    to_mirror(kv_over, True).wait_recv()
-    each(1, half_n, spread_over(kv_over), start)
-
+    pack_kv(in_b, rows // 2)
+    to_mirror(in_b, False).start()
+    to_mirror(in_a, True).wait_recv()
+    each(1, half_n, spread_over(in_a), start)
+    cuts = [half_n]
+    for share in FLOW:
+        cuts.append(min(n, cuts[-1] + share * half_n // 8))
+    early = EARLY * half_n // 8
+    each(half_n, half_n + early, far(in_b), start)
+    pack_kv(in_b, 0)
+    own_copy(in_b).start()
     f_q.wait()
-    lax.fori_loop(0, ch // tile, pack_rows(box_q, rows // 2, 0), 0)
-    to_mirror(q_over, False).start()
-    lax.fori_loop(0, ch // tile, pack_rows(box_q, 0, 0), 0)
-    own_q = pltpu.make_async_copy(slab(box_q, 0, cap), slab(arr_q, me, cap), self_sems.at[1])
-    own_q.start()
+    pack_rows(box_q, rows // 2, tiles, lambda c: c * tile)
+    to_mirror(in_q, False).start()
+    pack_rows(box_q, 0, tiles, lambda c: c * tile)
+    own_copy(in_q).start()
+    to_mirror(in_b, True).wait_recv()
+    each(1, half_n, spread_over(in_b), start)
     decay[...] = jnp.exp(-rate[...])
-    spans = scan_spans(n)
     sub = lax.broadcasted_iota(jnp.int32, (ROWS, 1), 0)
     first = jnp.logical_and(sub == 0, me > 0)
     later = ((ROWS - 1 - sub) * steps).astype(f32)
     segment = (sub * steps).astype(f32)
-    leap_of = {}
-    for k, span in enumerate(spans):
-        for j in range(1, 4):
-            if j * span < n:
-                for lag in (j * span - 1,) + ((j * span,) if k < len(spans) - 1 else ()):
-                    leap_of.setdefault(lag, len(leap_of))
-    for lag, at in leap_of.items():
-        leaps[at] = jnp.exp(-rate[...] * float(tok * lag))
+    member, level = me % QUAD, me // QUAD
+    levels = n // QUAD
+    share = poles // QUAD
+    for q in range(QUAD):
+        rate4[q] = rate[q * share : (q + 1) * share, :]
+    lags = [1, 2, 3] + [QUAD * j for j in range(1, levels - 1)]
+    for at, lag in enumerate(lags):
+        leaps[at] = jnp.exp(-rate4[member] * float(tok * lag))
     for at, by in enumerate((1, 2, 4)):
         hops[at] = jnp.exp(-rate[...] * float(steps * by))
 
@@ -679,77 +696,89 @@
     rim_want = jnp.where(rim_row < 2, rim_row + me * tok + tok - 2, -100).astype(f32)
     rim_hot = (rim_want == came_pos).astype(f32).astype(bf16)
 
-    to_mirror(q_over, True).wait_recv()
-    each(1, half_n, spread_over(q_over), start)
-    own_kv.wait()
-    each(1, half_n, near(kv_direct, True), arrive)
-    each(1, half_n, near(q_direct), start)
-    each(1, half_n, spread_over(kv_over, True), arrive)
-    cuts = [half_n]
-    for share in FLOW:
-        cuts.append(min(n, cuts[-1] + share * half_n // 8))
-    each(half_n, cuts[0] + n - cuts[1], far(kv_direct, True), arrive)
-    ahead = cuts[1] - half_n
-
-    def kv_then_q(m, c):
-        far(kv_direct, True)(m).wait_recv()
-        far(q_direct)(m - n + cuts[1]).start()
-        return c
-
-    lax.fori_loop(n - ahead, n, kv_then_q, 0)
-
-    def rim_copy(src, dst, k, to):
+    to_mirror(in_q, True).wait_recv()
+    each(1, half_n, spread_over(in_q), start)
+
+    def take_then_send(which, then, ahead, first_sent):
+        each(half_n, n - ahead, far(which, True), arrive)
+
+        def both(m, c):
+            far(which, True)(m).wait_recv()
+            far(then)(m - n + ahead + first_sent).start()
+            return c
+
+        lax.fori_loop(n - ahead, n, both, 0)
+
+    own_copy(in_a).wait()
+    each(1, half_n, near(in_a, True), arrive)
+    each(1, half_n, near(in_b), start)
+    each(1, half_n, spread_over(in_a, True), arrive)
+    take_then_send(in_a, in_b, half_n - early, half_n + early)
+
+    def rim_copy(i, to):
+        wide = (2 * (parts[i][1] - parts[i][0]) if i < len(parts) else tiles) * tile
+        cols = pl.ds((2 * parts[i][0] if i < len(parts) else 2 * tiles) * tile, wide)
         return pltpu.make_async_remote_copy(
-            src_ref=src, dst_ref=dst, send_sem=rim_sems.at[2 * k], recv_sem=rim_sems.at[2 * k + 1],
-            device_id={"ctx": to}, device_id_type=MESH,
+            src_ref=rims_out.at[:, cols], dst_ref=rims_in.at[:, cols], send_sem=rim_sems.at[2 * i],
+            recv_sem=rim_sems.at[2 * i + 1], device_id={"ctx": to}, device_id_type=MESH,
         )
 
     after, before = lax.rem(me + 1, n), lax.rem(me + n - 1, n)
 
-    def rim_tile(arr, rim):
+    def rim_send(i):
+        count = 2 * (parts[i][1] - parts[i][0]) if i < len(parts) else tiles
+        base_tile = 2 * parts[i][0] if i < len(parts) else 2 * tiles
+
         def fill(c, _):
-            cols = pl.ds(pl.multiple_of(c * tile, LANES), tile)
-            rim[:, cols] = jnp.dot(rim_hot, arr[:, cols], preferred_element_type=f32).astype(bf16)
+            src = pl.ds(pl.multiple_of(c * tile, LANES), tile)
+            dst = pl.ds(pl.multiple_of((base_tile + c) * tile, LANES), tile)
+            rims_out[:, dst] = jnp.dot(rim_hot, arrs[i][:, src], preferred_element_type=f32)[0:ROWS].astype(bf16)
             return _
 
-        return fill
-
-    lax.fori_loop(0, 2 * ch // tile, rim_tile(arr_kv, rim_kv_out), 0)
-    rim_kv = rim_copy(rim_kv_out, rim_kv_in, 0, after)
-    rim_kv.start()
+        lax.fori_loop(0, count, fill, 0)
+        rim_copy(i, after).start()
 
     def featured(arr, at, w_at):
         x = jnp.dot(place_s[...], arr[:, pl.ds(pl.multiple_of(at, LANES), tile)], preferred_element_type=f32)
         w = convw[:, pl.ds(pl.multiple_of(w_at, LANES), tile)]
         return w[0:1] * x[2 * ROWS :] + w[1:2] * x[ROWS : ROWS + tok] + w[2:3] * x[:tok]
 
-    def product_tile(c, _):
-        at = c * tile
-        k = featured(arr_kv, at, ch + at)
-        v = featured(arr_kv, ch + at, 2 * ch + at)
-        raw[:, pl.ds(pl.multiple_of(at, LANES), tile)] = k[: 2 * ROWS]
-        raw[:, pl.ds(pl.multiple_of(ch + at, LANES), tile)] = v[: 2 * ROWS]
-        prod[:, pl.ds(pl.multiple_of(at, LANES), tile)] = k * v
-        return _
-
-    lax.fori_loop(0, ch // tile, product_tile, 0)
-    each(cuts[1], cuts[2], far(q_direct), start)
-    rim_copy(rim_kv_out, rim_kv_in, 0, before).wait_recv()
-
-    def edge_tile(c, _):
-        def with_edge(at):
-            cols = pl.ds(pl.multiple_of(at, LANES), tile)
-            w = convw[:, pl.ds(pl.multiple_of(ch + at, LANES), tile)]
-            edge = rim_kv_in[:, cols].astype(f32)
-            top = jnp.where(first, w[1:2] * edge[1:2] + w[2:3] * edge[0:1], 0.0)
-            nxt = jnp.where(first, w[2:3] * edge[1:2], 0.0)
-            return jnp.concatenate([raw[0:ROWS, cols] + top, raw[ROWS:, cols] + nxt], axis=0)
-
-        at = c * tile
-        prod[0 : 2 * ROWS, pl.ds(pl.multiple_of(at, LANES), tile)] = with_edge(at) * with_edge(ch + at)
-        return _
-
-    lax.fori_loop(0, ch // tile, edge_tile, 0)
+    def product(i):
+        t0, t1 = parts[i]
+        wide = (t1 - t0) * tile
+
+        def product_tile(c, _):
+            at = (c - t0) * tile
+            k = featured(arrs[i], at, ch + c * tile)
+            v = featured(arrs[i], wide + at, 2 * ch + c * tile)
+            raw[:, pl.ds(pl.multiple_of(c * tile, LANES), tile)] = k[: 2 * ROWS]
+            raw[:, pl.ds(pl.multiple_of(ch + c * tile, LANES), tile)] = v[: 2 * ROWS]
+            prod[:, pl.ds(pl.multiple_of(c * tile, LANES), tile)] = k * v
+            return _
+
+        lax.fori_loop(t0, t1, product_tile, 0)
+
+    def product_edges(i):
+        t0, t1 = parts[i]
+        wide = (t1 - t0) * tile
+        rim_copy(i, before).wait_recv()
+
+        def edge_tile(c, _):
+            def with_edge(at, rim_at):
+                cols = pl.ds(pl.multiple_of(at, LANES), tile)
+                w = convw[:, pl.ds(pl.multiple_of(ch + at, LANES), tile)]
+                edge = rims_in[:, pl.ds(pl.multiple_of(rim_at, LANES), tile)].astype(f32)
+                top = jnp.where(first, w[1:2] * edge[1:2] + w[2:3] * edge[0:1], 0.0)
+                nxt = jnp.where(first, w[2:3] * edge[1:2], 0.0)
+                return jnp.concatenate([raw[0:ROWS, cols] + top, raw[ROWS:, cols] + nxt], axis=0)
+
+            rim_at = (2 * t0 + c - t0) * tile
+            prod[0 : 2 * ROWS, pl.ds(pl.multiple_of(c * tile, LANES), tile)] = with_edge(
+                c * tile, rim_at
+            ) * with_edge(ch + c * tile, rim_at + wide)
+            return _
+
+        lax.fori_loop(t0, t1, edge_tile, 0)
 
     def spread(ref, k, cols):
         return jnp.broadcast_to(ref[k : k + 1, cols], (ROWS, LANES))
@@ -788,57 +817,84 @@
             state[k, :, cols] = resid[k : k + 1, cols] * x
         return _
 
-    middle = (ch // LANES + 1) // 2
-    parts = [(0, middle), (middle, ch // LANES)]
-
-    def scan_copy(part, k, j, to):
-        cols = pl.ds(part[0] * LANES, (part[1] - part[0]) * LANES)
-        at = (3 * k + j - 1) * len(parts) + parts.index(part)
+    per = tile // LANES
+
+    def lanes(part):
+        return pl.ds(part[0] * tile, (part[1] - part[0]) * tile)
+
+    def scan_copy(part, stage, j, out_way):
+        cols = lanes(part)
+        here = member if stage != 1 else level
+        count = QUAD if stage != 1 else levels
+        peer = lax.rem(here + (j if out_way else count - j), count)
+        to = level * QUAD + peer if stage != 1 else peer * QUAD + member
+        start_at = stage * max(QUAD, levels)
+        source, slot = (totals.at[0, :, cols], start_at + here) if stage == 1 else (
+            tx.at[stage // 2 * QUAD + peer, :, cols], start_at + here)
+        if not out_way:
+            slot = start_at + peer
+        at = (start_at + j) * len(parts) + parts.index(part)
         return pltpu.make_async_remote_copy(
-            src_ref=tx.at[k, :, cols], dst_ref=rx.at[3 * k + j - 1, :, cols], send_sem=scan_send.at[at],
+            src_ref=source, dst_ref=rx.at[slot, :, cols], send_sem=scan_send.at[at],
             recv_sem=scan_recv.at[at], device_id={"ctx": to}, device_id_type=MESH,
         )
 
-    def scan_moves(part, k, send, act):
-        span = spans[k]
-        for j in range(1, 4):
-            if j * span < n:
-                to = me + j * span if send else me - j * span
-                act(scan_copy(part, k, j, lax.rem(to + n, n)))
-
-    def scan_start(part, k):
-        cols = pl.ds(part[0] * LANES, (part[1] - part[0]) * LANES)
-        tx[k, :, cols] = own[:, cols].astype(bf16)
-        scan_moves(part, k, True, start)
-
-    def scan_take(part, k):
-        span = spans[k]
-        cols = pl.ds(part[0] * LANES, (part[1] - part[0]) * LANES)
-        scan_moves(part, k, False, arrive)
-        for j in range(1, 4):
-            if j * span < n:
-                got = jnp.where(me >= j * span, rx[3 * k + j - 1, :, cols].astype(f32), 0.0)
-                acc[0, :, cols] = acc[0, :, cols] + leaps[leap_of[j * span - 1], :, cols] * got
-                if k < len(spans) - 1:
-                    own[:, cols] = own[:, cols] + leaps[leap_of[j * span], :, cols] * got
-
-    acc[0] = jnp.zeros((poles, ch), f32)
-    for part in parts:
-        lax.fori_loop(part[0], part[1], local_tile, 0)
-        scan_start(part, 0)
-    each(cuts[2], cuts[3], far(q_direct), start)
-    lax.fori_loop(0, ch // LANES, prefix_tile, 0)
-    for k in range(len(spans) - 1):
-        for part in parts:
-            scan_take(part, k)
-            scan_start(part, k + 1)
-    each(cuts[3], n, far(q_direct), start)
-
+    def scan_moves(part, stage, out_way, act):
+        for j in range(1, QUAD if stage != 1 else levels):
+            act(scan_copy(part, stage, j, out_way))
+
+    def leap(lag, cols):
+        return leaps[lags.index(lag), :, cols]
+
+    def scan_open(part):
+        cols = lanes(part)
+        for q in range(QUAD):
+            tx[q, :, cols] = own[q * share : (q + 1) * share, cols]
+        rx[member, :, cols] = tx[member, :, cols]
+        scan_moves(part, 0, True, start)
+
+    def scan_totals(part):
+        cols = lanes(part)
+        scan_moves(part, 0, False, arrive)
+        t = rx[QUAD - 1, :, cols]
+        for i in range(QUAD - 1):
+            t = t + leap(QUAD - 1 - i, cols) * rx[i, :, cols]
+        totals[0, :, cols] = t
+        scan_moves(part, 1, True, start)
+
+    def scan_carries(part):
+        cols = lanes(part)
+        scan_moves(part, 1, False, arrive)
+        carried = jnp.zeros((share, (part[1] - part[0]) * tile), f32)
+        for j in range(1, levels):
+            got = rx[max(QUAD, levels) + lax.rem(level + levels - j, levels), :, cols]
+            got = got if j == 1 else leap(QUAD * (j - 1), cols) * got
+            carried = carried + jnp.where(level >= j, got, 0.0)
+        for i in range(QUAD):
+            tx[QUAD + i, :, cols] = carried
+            carried = rx[i, :, cols] + leap(1, cols) * carried
+        rx[2 * max(QUAD, levels) + member, :, cols] = tx[QUAD + member, :, cols]
+        scan_moves(part, 2, True, start)
+
+    def scan_close(part):
+        cols = lanes(part)
+        scan_moves(part, 2, False, arrive)
+        for q in range(QUAD):
+            acc[q * share : (q + 1) * share, cols] = rx[2 * max(QUAD, levels) + q, :, cols]
+
+
+    def local(part):
+        lax.fori_loop(part[0] * per, part[1] * per, local_tile, 0)
+
+    def prefix(part):
+        lax.fori_loop(part[0] * per, part[1] * per, prefix_tile, 0)
+
+    part_a, part_b = parts
     def carry_tile(c, _):
         cols = pl.ds(pl.multiple_of(c * LANES, LANES), LANES)
         dec = [spread(decay, k, cols) for k in range(poles)]
         begin = tuple(
-            state[k, :, cols] + inward[k, :, cols] * acc[0, k : k + 1, cols] for k in range(poles)
+            state[k, :, cols] + inward[k, :, cols] * acc[k : k + 1, cols] for k in range(poles)
         )
 
         def step(i, g):
@@ -850,9 +906,37 @@
         lax.fori_loop(0, steps, step, begin, unroll=4)
         return _
 
-    for part in parts:
-        scan_take(part, len(spans) - 1)
-        lax.fori_loop(part[0], part[1], carry_tile, 0)
+    def carry(part):
+        scan_close(part)
+        lax.fori_loop(part[0] * per, part[1] * per, carry_tile, 0)
+
+    rim_send(in_a)
+    product(in_a)
+    product_edges(in_a)
+    local(part_a)
+    scan_open(part_a)
+    prefix(part_a)
+    own_copy(in_b).wait()
+    each(1, half_n, near(in_b, True), arrive)
+    each(1, half_n, near(in_q), start)
+    each(half_n, cuts[1], far(in_q), start)
+    scan_totals(part_a)
+    each(1, half_n, spread_over(in_b, True), arrive)
+    take_then_send(in_b, in_q, cuts[2] - cuts[1], cuts[1])
+    rim_send(in_b)
+    scan_carries(part_a)
+    product(in_b)
+    each(cuts[2], cuts[3], far(in_q), start)
+    product_edges(in_b)
+    local(part_b)
+    scan_open(part_b)
+    each(cuts[3], cuts[4], far(in_q), start)
+    prefix(part_b)
+    scan_totals(part_b)
+    carry(part_a)
+    each(cuts[4], n, far(in_q), start)
+    scan_carries(part_b)
+    carry(part_b)
     top_of = worst
     for g in range(1, groups):
         group_copy(g, lax.rem(group + groups - g, groups)).wait_recv()
@@ -860,13 +944,11 @@
     most[0] = jnp.max(top_of).astype(jnp.int32)
     w_copy.wait()
 
-    own_q.wait()
-    each(1, half_n, near(q_direct, True), arrive)
-    each(1, half_n, spread_over(q_over, True), arrive)
-    each(half_n, n, far(q_direct, True), arrive)
-    lax.fori_loop(0, ch // tile, rim_tile(arr_q, rim_q_out), 0)
-    rim_q = rim_copy(rim_q_out, rim_q_in, 1, after)
-    rim_q.start()
+    own_copy(in_q).wait()
+    each(1, half_n, near(in_q, True), arrive)
+    each(1, half_n, spread_over(in_q, True), arrive)
+    each(half_n, n, far(in_q, True), arrive)
+    rim_send(in_q)
 
     def gate_tile(c, _):
         at = c * tile
@@ -877,8 +959,8 @@
         return _
 
     lax.fori_loop(0, ch // tile, gate_tile, 0)
-    rim_copy(rim_q_out, rim_q_in, 1, before).wait_recv()
-    edge = rim_q_in[...].astype(f32)
+    rim_copy(in_q, before).wait_recv()
+    edge = rims_in[:, 2 * ch :].astype(f32)
     w1, w2 = convw[1:2, 0:ch], convw[2:3, 0:ch]
     top = jnp.where(first, w1 * edge[1:2] + w2 * edge[0:1], 0.0)
     nxt = jnp.where(first, w2 * edge[1:2], 0.0)
@@ -903,20 +985,20 @@
 
     lax.fori_loop(0, ch // tile, out_tile, 0)
 
-    for which in (kv_direct, q_direct):
+    for which in (in_a, in_b, in_q):
         each(1, half_n, near(which), sent)
         each(half_n, n, far(which), sent)
-    for which in (kv_over, q_over):
+    for which in (in_a, in_b, in_q):
         to_mirror(which, False).wait_send()
         each(1, half_n, spread_over(which), sent)
     each(1, n, lambda m: marks_to(m, flip(me, m), me), sent)
     for g in range(1, groups):
         group_copy(g, lax.rem(group + g, groups)).wait_send()
-    rim_kv.wait_send()
-    rim_q.wait_send()
-    for k in range(len(spans)):
+    for which in (in_a, in_b, in_q):
+        rim_copy(which, after).wait_send()
+    for stage in range(3):
         for part in parts:
-            scan_moves(part, k, True, sent)
+            scan_moves(part, stage, True, sent)
 
 
 def swift_call(n, groups, cap, base, tok, args):
@@ -925,7 +1007,9 @@
     ch = feat // 3
     poles = pole_rate.shape[0]
     rows = n * cap
-    stages = len(scan_spans(n))
+    share = poles // QUAD
+    wide = max(QUAD, n // QUAD)
+    lead = (ch // col_tile(ch) + 1) // 2 * col_tile(ch)
     whole = pl.BlockSpec(memory_space=pltpu.VMEM)
     dma = pltpu.SemaphoreType.DMA
     vmem = pltpu.VMEM
@@ -936,9 +1020,11 @@
         + [whole] * 5 + [pl.BlockSpec(memory_space=pl.ANY)],
         out_specs=(whole, pl.BlockSpec(memory_space=pltpu.SMEM)),
         scratch_shapes=[
-            vmem((rows, 2 * ch), bf16),
+            vmem((rows, 2 * lead), bf16),
+            vmem((rows, 2 * (ch - lead)), bf16),
             vmem((rows, ch), bf16),
-            vmem((rows, 2 * ch), bf16),
+            vmem((rows, 2 * lead), bf16),
+            vmem((rows, 2 * (ch - lead)), bf16),
             vmem((rows, ch), bf16),
             vmem((n, 2, LANES), f32),
             vmem((n, 2, LANES), f32),
@@ -953,27 +1039,23 @@
             vmem((poles, ROWS, ch), f32),
             vmem((slots, feat), bf16),
             vmem((poles, ch), f32),
-            vmem((16, 2 * ch), bf16),
-            vmem((16, 2 * ch), bf16),
-            vmem((16, ch), bf16),
-            vmem((16, ch), bf16),
+            vmem((ROWS, feat), bf16),
+            vmem((ROWS, feat), bf16),
             vmem((poles, ch), f32),
-            vmem((1, poles, ch), f32),
-            vmem((stages, poles, ch), bf16),
-            vmem((3 * stages, poles, ch), bf16),
+            vmem((poles, ch), f32),
+            vmem((1, share, ch), f32),
+            vmem((QUAD, share, ch), f32),
+            vmem((2 * QUAD, share, ch), f32),
+            vmem((3 * wide, share, ch), f32),
             vmem(out_weight.shape, bf16),
-        ]
-        + [dma((n,))] * 6
-        + [dma((groups,))] * 2
-        + [dma((n,))] * 4
-        + [
+            dma((3, n)), dma((3, n)), dma((3, n)), dma((3, n)), dma((n,)), dma((n,)), dma((groups,)), dma((groups,)),
             vmem((2 * ROWS, 2 * ch), f32),
             vmem((poles, ROWS, ch), f32),
             vmem((poles, ROWS, ch), f32),
             vmem((3, poles, ch), f32),
-            vmem((6 * stages, poles, ch), f32),
-        ]
-        + [dma((4,)), dma((6 * stages,)), dma((6 * stages,)), dma((2,)), dma, dma((2,))],
+            vmem((2 + n // QUAD, share, ch), f32),
+            dma((6,)), dma((6 * wide,)), dma((6 * wide,)), dma((3,)), dma, dma((2,)),
+        ],
         compiler_params=pltpu.CompilerParams(
             collective_id=1, has_side_effects=True, vmem_limit_bytes=60 << 20
         ),
@@ -1038,20 +1120,23 @@
     ch = feat // 3
     tok = 2 * slots // 3
     cap = 2 * tok // n
+    poles = pole_rate.shape[0]
     if cap % 16 or tok & (tok - 1) or tok > 256 or conv_weight.shape[0] != 3 or ch % LANES or n & (n - 1) or n < 4:
         return plain_on_device(
             features, positions, counts, conv_weight, pole_rate, pole_residue, skip_gain, out_weight
         )
     args = (counts, features, positions, conv_weight, pole_rate, pole_residue, skip_gain, out_weight)
     base = slots // n
-    if base % ROWS or cap - base > 16 or LANES % cap:
+    if poles % QUAD or base % ROWS or cap - base > 16 or LANES % cap:
         return mega_call(n, cap, tok, args)
     done, most = swift_call(n, groups, cap, base, tok, args)
     return lax.cond(most[0] > cap - base, lambda d: mega_call(n, cap, tok, args), lambda d: d, done)
 
 
 PACE = (2, 1, 1, 2, 2)
-FLOW = (4, 2, 1)
+FLOW = (3, 2, 1, 1)
+EARLY = 0
+QUAD = 4
 
 
 def solution(mesh):

time: 137 us -> 135 us (0.985)
  Pallas kernels: 134 us -> 132 us
    pallas_call x1, Pallas kernels: 134 us -> 132 us  [swift_call(): pl.pallas_call(functools.partial(swift, n, groups, cap, base, tok), out_s...]
where the time goes in v3:
time: 135 us; the launch traced here: 134 us
  Pallas kernels  132 us (98%)
    pallas_call x1, Pallas kernels, swift_call(): pl.pallas_call(functools.partial(swift, n, groups, cap, base, tok), out_s...  132 us

profile of v3, /device:TPU:0, one launch (start us, length us, event | category | flops | bytes accessed | tf_op | source)
XLA Modules:
  0.0 134.4 jit_solution(7247029898430756887)
XLA Ops:
  0.0 0.0 copy-start.3
  0.0 0.0 copy-start.1
  0.0 0.0 copy-start
  0.0 0.0 copy-start.2
  0.0 0.0 copy-start.4
  0.7 132.1 %hyena_direct.1 = (bf16[256,1920]{1,0:T(8,128)(2,1)S(1)}, s32[1]{0:T(128)}) custom-call(s32[1]{0:T(128)S(6)} %copy.14.counts, bf16[384,5760]{1,0:T(8,128)(2,1)} %feats_hbm.1, s32[384]{0:T(512)} %pos.1, f32[3,5760]{1,0:T(4,128)} %convw.1, f32[16,1920]{1,0:T(8,128)} %rate.1, f32[16,1920]{1,0:T(8,128)} %resid.1, f32[1920]{0:T(1024)} %skip.1, ...), custom_call_target="tpu_custom_call" | custom-call | tf_op jit(solution)/shard_map/hyena_direct/pallas_call | solution.py:1016
  133.4 0.0 copy-done.3
  133.4 0.0 copy-done.1
  133.4 0.0 copy-done
  133.4 0.0 copy-done.2
  133.4 0.0 copy-done.4
  133.5 0.9 copy.15
  (1 shorter events, 0.0 us)
Async XLA Ops:
  0.0 133.4 %copy-start.3 = (f32[1920]{0:T(1024)S(1)}, f32[1920]{0:T(1024)}, u32[]{:S(2)}) copy-start(f32[1920]{0:T(1024)} %skip.1) | copy-start | bytes 23044
  0.0 133.4 %copy-start.1 = (f32[16,1920]{1,0:T(8,128)S(1)}, f32[16,1920]{1,0:T(8,128)}, u32[]{:S(2)}) copy-start(f32[16,1920]{1,0:T(8,128)} %resid.1) | copy-start | bytes 368644
  0.0 133.4 %copy-start = (f32[16,1920]{1,0:T(8,128)S(1)}, f32[16,1920]{1,0:T(8,128)}, u32[]{:S(2)}) copy-start(f32[16,1920]{1,0:T(8,128)} %rate.1) | copy-start | bytes 368644
  0.0 133.4 %copy-start.2 = (f32[3,5760]{1,0:T(4,128)S(1)}, f32[3,5760]{1,0:T(4,128)}, u32[]{:S(2)}) copy-start(f32[3,5760]{1,0:T(4,128)} %convw.1) | copy-start | bytes 207364
  0.0 133.4 %copy-start.4 = (s32[384]{0:T(512)S(1)}, s32[384]{0:T(512)}, u32[]{:S(2)}) copy-start(s32[384]{0:T(512)} %pos.1) | copy-start | bytes 4612

commit v4 on v3

--- a/solution.py
+++ b/solution.py
@@ -920,11 +920,10 @@
     each(1, half_n, near(in_b, True), arrive)
     each(1, half_n, near(in_q), start)
     each(half_n, cuts[1], far(in_q), start)
-    scan_totals(part_a)
     each(1, half_n, spread_over(in_b, True), arrive)
     take_then_send(in_b, in_q, cuts[2] - cuts[1], cuts[1])
     rim_send(in_b)
-    scan_carries(part_a)
+    scan_totals(part_a)
     product(in_b)
     each(cuts[2], cuts[3], far(in_q), start)
     product_edges(in_b)
@@ -932,9 +931,10 @@
     scan_open(part_b)
     each(cuts[3], cuts[4], far(in_q), start)
     prefix(part_b)
+    scan_carries(part_a)
     scan_totals(part_b)
+    each(cuts[4], n, far(in_q), start)
     carry(part_a)
-    each(cuts[4], n, far(in_q), start)
     scan_carries(part_b)
     carry(part_b)
     top_of = worst
@@ -978,12 +978,14 @@
 
     lax.fori_loop(0, ch // tile, order_tile, 0)
 
+    wide = 640 if ch % 640 == 0 else tile
+
     def out_tile(c, _):
-        cols = pl.ds(pl.multiple_of(c * tile, LANES), tile)
+        cols = pl.ds(pl.multiple_of(c * wide, LANES), wide)
         out[:, cols] = jnp.dot(natural[...], w_vmem[:, cols], preferred_element_type=f32).astype(bf16)
         return _
 
-    lax.fori_loop(0, ch // tile, out_tile, 0)
+    lax.fori_loop(0, ch // wide, out_tile, 0)
 
     for which in (in_a, in_b, in_q):
         each(1, half_n, near(which), sent)
@@ -1134,7 +1136,7 @@
 
 
 PACE = (2, 1, 1, 2, 2)
-FLOW = (3, 2, 1, 1)
+FLOW = (0, 2, 1, 1)
 EARLY = 0
 QUAD = 4
 

time: 135 us -> 130 us (0.963)
  Pallas kernels: 132 us -> 128 us
    pallas_call x1, Pallas kernels: 132 us -> 128 us  [swift_call(): pl.pallas_call(functools.partial(swift, n, groups, cap, base, tok), out_s...]
where the time goes in v4:
time: 130 us
  Pallas kernels  128 us (98%)
  between operations  1.32 us (1%)
    pallas_call x1, Pallas kernels, swift_call(): pl.pallas_call(functools.partial(swift, n, groups, cap, base, tok), out_s...  128 us

profile of v4, /device:TPU:0, one launch (start us, length us, event | category | flops | bytes accessed | tf_op | source)
XLA Modules:
  0.0 130.0 jit_solution(7061738885430794335)
XLA Ops:
  0.0 0.0 copy-start.3
  0.0 0.0 copy-start.1
  0.0 0.0 copy-start
  0.0 0.0 copy-start.2
  0.0 0.0 copy-start.4
  0.7 127.7 %hyena_direct.1 = (bf16[256,1920]{1,0:T(8,128)(2,1)S(1)}, s32[1]{0:T(128)}) custom-call(s32[1]{0:T(128)S(6)} %copy.14.counts, bf16[384,5760]{1,0:T(8,128)(2,1)} %feats_hbm.1, s32[384]{0:T(512)} %pos.1, f32[3,5760]{1,0:T(4,128)} %convw.1, f32[16,1920]{1,0:T(8,128)} %rate.1, f32[16,1920]{1,0:T(8,128)} %resid.1, f32[1920]{0:T(1024)} %skip.1, ...), custom_call_target="tpu_custom_call" | custom-call | tf_op jit(solution)/shard_map/hyena_direct/pallas_call | solution.py:1018
  128.9 0.0 copy-done.3
  129.0 0.0 copy-done.1
  129.0 0.0 copy-done
  129.0 0.0 copy-done.2
  129.0 0.0 copy-done.4
  129.0 0.9 copy.15
  (1 shorter events, 0.0 us)
Async XLA Ops:
  0.0 128.9 %copy-start.3 = (f32[1920]{0:T(1024)S(1)}, f32[1920]{0:T(1024)}, u32[]{:S(2)}) copy-start(f32[1920]{0:T(1024)} %skip.1) | copy-start | bytes 23044
  0.0 129.0 %copy-start.1 = (f32[16,1920]{1,0:T(8,128)S(1)}, f32[16,1920]{1,0:T(8,128)}, u32[]{:S(2)}) copy-start(f32[16,1920]{1,0:T(8,128)} %resid.1) | copy-start | bytes 368644
  0.0 129.0 %copy-start = (f32[16,1920]{1,0:T(8,128)S(1)}, f32[16,1920]{1,0:T(8,128)}, u32[]{:S(2)}) copy-start(f32[16,1920]{1,0:T(8,128)} %rate.1) | copy-start | bytes 368644
  0.0 129.0 %copy-start.2 = (f32[3,5760]{1,0:T(4,128)S(1)}, f32[3,5760]{1,0:T(4,128)}, u32[]{:S(2)}) copy-start(f32[3,5760]{1,0:T(4,128)} %convw.1) | copy-start | bytes 207364
  0.0 129.0 %copy-start.4 = (s32[384]{0:T(512)S(1)}, s32[384]{0:T(512)}, u32[]{:S(2)}) copy-start(s32[384]{0:T(512)} %pos.1) | copy-start | bytes 4612

commit v5 on v4

--- a/solution.py
+++ b/solution.py
@@ -710,8 +710,8 @@
         lax.fori_loop(n - ahead, n, both, 0)
 
     own_copy(in_a).wait()
+    each(1, half_n, near(in_b), start)
     each(1, half_n, near(in_a, True), arrive)
-    each(1, half_n, near(in_b), start)
     each(1, half_n, spread_over(in_a, True), arrive)
     take_then_send(in_a, in_b, half_n - early, half_n + early)
 
@@ -933,9 +933,10 @@
     prefix(part_b)
     scan_carries(part_a)
     scan_totals(part_b)
-    each(cuts[4], n, far(in_q), start)
+    each(cuts[4], cuts[5], far(in_q), start)
     carry(part_a)
     scan_carries(part_b)
+    each(cuts[5], n, far(in_q), start)
     carry(part_b)
     top_of = worst
     for g in range(1, groups):
@@ -1136,7 +1137,7 @@
 
 
 PACE = (2, 1, 1, 2, 2)
-FLOW = (0, 2, 1, 1)
+FLOW = (0, 2, 1, 1, 2)
 EARLY = 0
 QUAD = 4
 

time: 130 us -> 130 us (level)
  no operation moved by 1% of the time
where the time goes in v5:
time: 130 us; the launch traced here: 129 us
  Pallas kernels  127 us (98%)
  between operations  1.32 us (1%)
    pallas_call x1, Pallas kernels, swift_call(): pl.pallas_call(functools.partial(swift, n, groups, cap, base, tok), out_s...  127 us

profile of v5, /device:TPU:0, one launch (start us, length us, event | category | flops | bytes accessed | tf_op | source)
XLA Modules:
  0.0 129.2 jit_solution(3035557442017089544)
XLA Ops:
  0.0 0.0 copy-start.3
  0.0 0.0 copy-start.1
  0.0 0.0 copy-start
  0.0 0.0 copy-start.2
  0.0 0.0 copy-start.4
  0.7 126.9 %hyena_direct.1 = (bf16[256,1920]{1,0:T(8,128)(2,1)S(1)}, s32[1]{0:T(128)}) custom-call(s32[1]{0:T(128)S(6)} %copy.14.counts, bf16[384,5760]{1,0:T(8,128)(2,1)} %feats_hbm.1, s32[384]{0:T(512)} %pos.1, f32[3,5760]{1,0:T(4,128)} %convw.1, f32[16,1920]{1,0:T(8,128)} %rate.1, f32[16,1920]{1,0:T(8,128)} %resid.1, f32[1920]{0:T(1024)} %skip.1, ...), custom_call_target="tpu_custom_call" | custom-call | tf_op jit(solution)/shard_map/hyena_direct/pallas_call | solution.py:1019
  128.2 0.0 copy-done.3
  128.2 0.0 copy-done.1
  128.2 0.0 copy-done
  128.2 0.0 copy-done.2
  128.3 0.0 copy-done.4
  128.3 0.9 copy.15
  (1 shorter events, 0.0 us)
Async XLA Ops:
  0.0 128.2 %copy-start.3 = (f32[1920]{0:T(1024)S(1)}, f32[1920]{0:T(1024)}, u32[]{:S(2)}) copy-start(f32[1920]{0:T(1024)} %skip.1) | copy-start | bytes 23044
  0.0 128.2 %copy-start.1 = (f32[16,1920]{1,0:T(8,128)S(1)}, f32[16,1920]{1,0:T(8,128)}, u32[]{:S(2)}) copy-start(f32[16,1920]{1,0:T(8,128)} %resid.1) | copy-start | bytes 368644
  0.0 128.2 %copy-start = (f32[16,1920]{1,0:T(8,128)S(1)}, f32[16,1920]{1,0:T(8,128)}, u32[]{:S(2)}) copy-start(f32[16,1920]{1,0:T(8,128)} %rate.1) | copy-start | bytes 368644
  0.0 128.2 %copy-start.2 = (f32[3,5760]{1,0:T(4,128)S(1)}, f32[3,5760]{1,0:T(4,128)}, u32[]{:S(2)}) copy-start(f32[3,5760]{1,0:T(4,128)} %convw.1) | copy-start | bytes 207364
  0.0 128.2 %copy-start.4 = (s32[384]{0:T(512)S(1)}, s32[384]{0:T(512)}, u32[]{:S(2)}) copy-start(s32[384]{0:T(512)} %pos.1) | copy-start | bytes 4612
